TPU v7x, 32 devices: a whole 2x2x4 slice. The times are simulated.
32 devices in a mesh: section: 2 (over x), dp: 16 (over z, y, core).
Axes of the slice: x: 2, y: 2, z: 4, core: 2. Of those that a mesh axis runs over, the one named last changes fastest.
Arguments:
- saved_input: bfloat16 [2, 6144, 4096], P('section', 'dp'), may hold values from -8 to 8
- out_grad: bfloat16 [2, 6144, 768], P('section', 'dp'), may hold values from -8 to 8
- key_weight: bfloat16 [2, 4096, 768], P('section'), may hold values from -0.09375 to 0.09375
- layer_gate: float32 [2, 4096], P('section'), may hold values from 0.75 to 1
- q_prev: float32 [2, 768, 32], P('section'), may hold values from -0.21875 to 0.21875
- error_prev: bfloat16 [2, 16, 4096, 768], P('section', 'dp'), may hold values from -4 to 4
Outputs:
- upstream: bfloat16 [2, 6144, 4096], P('section', 'dp')
- p_basis: float32 [2, 4096, 32], P('section')
- q_factor: float32 [2, 768, 32], P('section')
- error_next: bfloat16 [2, 16, 4096, 768], P('section', 'dp')
All inputs are finite; a program needn't handle non-finite values.
Results may differ from a plain program's by a relative error of at most 0.0034.
Values may be sent and summed in bfloat16 or wider, within the bound.
No kernel may reach another device: no remote copies, remote signals or barrier semaphores. Data moves between devices by JAX's collectives and lax.ppermute only.
A program may use at most 192 MiB of HBM per device.

v0:
```python
import math

import jax
import jax.numpy as jnp
from jax import lax
from jax.sharding import PartitionSpec as P

highest = lax.Precision.HIGHEST


def shifted(block, axis, distance):
    devices = range(lax.axis_size(axis))
    route = [(i - distance, i) for i in devices if i - distance in devices]
    return lax.ppermute(block, axis, route)


def factor_rows(p_rows, gram_matrix):
    triangle = jnp.linalg.cholesky(gram_matrix)
    return lax.linalg.triangular_solve(
        triangle, p_rows, left_side=False, lower=True, transpose_a=True
    )


def key_branch(grad_block, weight_block):
    return lax.dot_general(
        grad_block, weight_block, (((1,), (1,)), ((), ())), preferred_element_type=jnp.float32
    )


def body(saved_input, out_grad, key_weight, layer_gate, q_prev, error_prev):
    inputs = saved_input[0]
    grads = out_grad[0]
    weights = key_weight[0]
    gate_row = layer_gate[0]
    right_prev = q_prev[0]
    replicas = lax.axis_size("dp")
    norm_scale = 1.0 / math.sqrt(inputs.shape[0])
    branch = key_branch(grads, weights)
    current = (gate_row[None, :] * branch).astype(jnp.bfloat16)
    received = shifted(current, "section", -1)
    current = (gate_row[None, :] * (branch + received.astype(jnp.float32))).astype(jnp.bfloat16)
    merged = (
        lax.dot_general(inputs, grads, (((0,), (0,)), ((), ())), preferred_element_type=jnp.float32)
        * norm_scale
    )
    merged = merged + error_prev[0, 0].astype(jnp.float32)
    local_left = jnp.dot(merged, right_prev, precision=highest)
    p_mean = lax.psum(local_left, "dp") / replicas
    gram_matrix = jnp.dot(p_mean.T, p_mean, precision=highest)
    basis = factor_rows(p_mean, gram_matrix)
    local_right = lax.dot_general(merged, basis, (((0,), (0,)), ((), ())), precision=highest)
    right_mean = lax.psum(local_right, "dp") / replicas
    approx = jnp.dot(basis, right_mean.T, precision=highest)
    error_next = (merged - approx).astype(jnp.bfloat16)
    return (current[None], basis[None], right_mean[None], error_next[None, None])


def solution(mesh):
    return jax.shard_map(
        body,
        mesh=mesh,
        in_specs=(
            P("section", "dp", None),
            P("section", "dp", None),
            P("section", None, None),
            P("section", None),
            P("section", None, None),
            P("section", "dp", None, None),
        ),
        out_specs=(
            P("section", "dp", None),
            P("section", None, None),
            P("section", None, None),
            P("section", "dp", None, None),
        ),
        check_vma=False,
    )
```

profile of v0, /device:TPU:0, one launch (start us, length us, event | category | flops | bytes accessed | tf_op | source)
XLA Modules:
  0.0 276.5 jit_solution(12295773977041552516)
XLA Ops:
  7.2 0.0 copy-start
  7.2 0.0 all-reduce.3.cloned.1.call-start
  7.2 0.0 copy-start.2
  7.2 0.0 copy-start.4
  7.2 9.4 %multiply_convert_fusion.1 = (bf16[384,4096]{1,0:T(8,128)(2,1)}, f32[384,4096]{1,0:T(8,128)}) fusion(f32[4096]{0:T(1024)} %bitcast.43, bf16[1,4096,768]{2,1,0:T(8,128)(2,1)} %param.8, bf16[1,384,768]{2,1,0:T(8,128)(2,1)} %param.7), kind=kOutput, calls=%fused_computation.5 | convolution fusion | flops 2419064832 | bytes 16334848 | tf_op jit(solution)/shard_map/dot_general | solution.py:25
  16.6 0.0 copy-start.6
  16.6 1.4 collective-permute-start
  18.1 0.0 copy-done
  18.1 0.0 copy-done.2
  18.1 0.0 copy-done.4
  18.1 3.5 %convert_add_fusion = f32[4096,768]{1,0:T(8,128)S(1)} fusion(bf16[1,1,4096,768]{3,2,1,0:T(8,128)(2,1)S(1)} %copy-done.2, bf16[1,384,4096]{2,1,0:T(8,128)(2,1)S(1)} %copy-done, bf16[1,384,768]{2,1,0:T(8,128)(2,1)S(1)} %copy-done.4), kind=kOutput, calls=%fused_computation | convolution fusion | flops 2425356288 | bytes 22609920 | tf_op jit(solution)/shard_map/dot_general | solution.py:43
  21.6 0.0 copy-start.1
  21.6 4.5 %copy-done.1 = f32[4096,768]{1,0:T(8,128)} copy-done((f32[4096,768]{1,0:T(8,128)}, f32[4096,768]{1,0:T(8,128)S(1)}, u32[]{:S(2)}) %copy-start.1) | copy-done | bytes 12582936
  26.1 0.0 copy-done.6
  26.1 12.5 %fusion.13 = f32[4096,32]{0,1:T(8,128)} fusion(f32[4096,768]{1,0:T(8,128)S(1)} %convert_add_fusion, f32[1,768,32]{1,2,0:T(8,128)S(1)} %copy-done.6), kind=kOutput, calls=%fused_computation.17 | convolution fusion | flops 1207959552 | bytes 13205504 | tf_op jit(solution)/shard_map/dot_general | solution.py:47
  38.7 0.0 all-reduce.3.cloned.1.call-update
  38.7 0.0 all-reduce.5.cloned.1.call-start
  38.7 96.3 %all-reduce.3.cloned.1.call-done = f32[4096,32]{0,1:T(8,128)} async-done(((f32[4096,32]{0,1:T(8,128)}), f32[4096,32]{0,1:T(8,128)}) %all-reduce.3.cloned.1.call-update) | async-done | bytes 524304 | tf_op jit(solution)/shard_map/psum | solution.py:48
  135.0 1.8 fusion.9
  136.8 0.1 copy.10
  136.9 2.9 %cholesky.16 = f32[32,32]{1,0:T(8,128)S(1)} custom-call(f32[32,32]{1,0:T(8,128)S(1)} %fusion.19), custom_call_target="Cholesky" | custom-call | tf_op jit(solution)/shard_map/jit(cholesky)/cholesky | solution.py:18
  139.9 0.6 compare_reduce_fusion
  140.5 0.7 fusion.17
  141.2 2.4 custom-call.6
  143.6 1.7 fusion.7
  145.3 0.0 copy-start.3
  145.3 0.8 copy-done.3
  146.1 11.1 %fusion.23 = f32[768,32]{0,1:T(8,128)} fusion(f32[4096,768]{1,0:T(8,128)} %copy-done.1, f32[4096,32]{0,1:T(8,128)S(1)} %fusion.7), kind=kOutput, calls=%fused_computation.34 | convolution fusion | flops 1207959552 | bytes 13205504 | tf_op jit(solution)/shard_map/dot_general | solution.py:51
  157.2 0.0 all-reduce.5.cloned.1.call-update
  157.2 89.3 %all-reduce.5.cloned.1.call-done = f32[768,32]{0,1:T(8,128)} async-done(((f32[768,32]{0,1:T(8,128)}), f32[768,32]{0,1:T(8,128)}) %all-reduce.5.cloned.1.call-update) | async-done | bytes 98320 | tf_op jit(solution)/shard_map/psum | solution.py:52
  246.6 1.5 multiply_bitcast_fusion
  248.1 0.0 copy-start.5
  248.1 15.1 %fusion.2 = bf16[1,1,4096,768]{3,2,1,0:T(8,128)(2,1)} fusion(f32[4096,768]{1,0:T(8,128)} %copy-done.1, f32[4096,32]{0,1:T(8,128)} %copy-done.3, f32[768,32]{0,1:T(8,128)} %all-reduce.5.cloned.1.call-done), kind=kOutput, calls=%fused_computation.6 | convolution fusion | flops 1214275584 | bytes 19496960 | tf_op jit(solution)/shard_map/dot_general | solution.py:53
  263.2 0.0 collective-permute-done
  263.2 0.0 copy-done.5
  263.2 6.4 %fusion.3 = bf16[1,384,4096]{2,1,0:T(8,128)(2,1)} fusion(f32[384,4096]{1,0:T(8,128)} %get-tuple-element.5, bf16[384,4096]{1,0:T(8,128)(2,1)} %collective-permute-done, f32[4096]{0:T(1024)S(1)} %bitcast.44), kind=kLoop, calls=%fused_computation.7 | loop fusion | flops 6291456 | bytes 12599296 | tf_op jit(solution)/shard_map/broadcast_in_dim | solution.py:55
  (2 shorter events, 0.0 us)
Async XLA Ops:
  7.2 10.9 %copy-start = (bf16[1,384,4096]{2,1,0:T(8,128)(2,1)S(1)}, bf16[1,384,4096]{2,1,0:T(8,128)(2,1)}, u32[]{:S(2)}) copy-start(bf16[1,384,4096]{2,1,0:T(8,128)(2,1)} %param.6) | copy-start | bytes 9437188
  7.2 127.9 %all-reduce.3.cloned.1.call-start = ((), (), s32[]{:S(2)}) async-start(), calls=%async_computation | async-start | bytes 1048576 | tf_op jit(solution)/shard_map/psum | solution.py:48
  7.2 10.9 %copy-start.2 = (bf16[1,1,4096,768]{3,2,1,0:T(8,128)(2,1)S(1)}, bf16[1,1,4096,768]{3,2,1,0:T(8,128)(2,1)}, u32[]{:S(2)}) copy-start(bf16[1,1,4096,768]{3,2,1,0:T(8,128)(2,1)} %param.11) | copy-start | bytes 18874372
  7.2 10.9 %copy-start.4 = (bf16[1,384,768]{2,1,0:T(8,128)(2,1)S(1)}, bf16[1,384,768]{2,1,0:T(8,128)(2,1)}, u32[]{:S(2)}) copy-start(bf16[1,384,768]{2,1,0:T(8,128)(2,1)} %param.7) | copy-start | bytes 1769476
  16.6 9.5 %copy-start.6 = (f32[1,768,32]{1,2,0:T(8,128)S(1)}, f32[1,768,32]{1,2,0:T(8,128)}, u32[]{:S(2)}) copy-start(f32[1,768,32]{1,2,0:T(8,128)} %param.10) | copy-start | bytes 294916
  16.6 246.5 %collective-permute-start = (bf16[384,4096]{1,0:T(8,128)(2,1)}, bf16[384,4096]{1,0:T(8,128)(2,1)}, u32[]{:S(2)}, u32[]{:S(2)}) collective-permute-start(bf16[384,4096]{1,0:T(8,128)(2,1)} %get-tuple-element.4), channel_id=1, source_target_pairs={{16,0},{17,1},{18,2},{19,3},{20,4},{21,5},{22,6},{23,7},{24,8},{25... | collective-permute-start | bytes 9437192 | tf_op jit(solution)/shard_map/ppermute | solution.py:14
  21.6 4.6 %copy-start.1 = (f32[4096,768]{1,0:T(8,128)}, f32[4096,768]{1,0:T(8,128)S(1)}, u32[]{:S(2)}) copy-start(f32[4096,768]{1,0:T(8,128)S(1)} %convert_add_fusion) | copy-start | bytes 37748740
  38.7 207.9 %all-reduce.5.cloned.1.call-start = ((), (), s32[]{:S(2)}) async-start(), calls=%async_computation.1 | async-start | bytes 196608 | tf_op jit(solution)/shard_map/psum | solution.py:52
  145.3 0.8 copy-start.3
  248.1 15.1 %copy-start.5 = (f32[1,4096]{1,0:T(1,128)S(1)}, f32[1,4096]{1,0:T(1,128)}, u32[]{:S(2)}) copy-start(f32[1,4096]{1,0:T(1,128)} %param.9) | copy-start | bytes 49156
Sparse Core Ops, SparseCore 0:
  38.8 96.1 all-reduce.2
  157.4 89.1 all-reduce.4
where the time goes:
time: 277 us; the launch traced here: 276 us
  waiting for transfers between devices  186 us (67%)
  matrix products  55.1 us (20%)
  other arithmetic  14.6 us (5%)
  between operations  14.2 us (5%)
  local copies, waits for them, and re-layouts  5.43 us (2%)
    psum x1, waiting for transfers between devices, body(): p_mean = lax.psum(local_left, 'dp') / replicas  96.3 us
    psum x1, waiting for transfers between devices, body(): right_mean = lax.psum(local_right, 'dp') / replicas  89.3 us
    dot_general x1, matrix products, body(): approx = jnp.dot(basis, right_mean.T, precision=highest)  15.1 us
    dot_general x1, matrix products, body(): local_left = jnp.dot(merged, right_prev, precision=highest)  12.5 us
    dot_general x1, matrix products, body(): lax.dot_general(merged, basis, (((0,), (0,)), ((), ())), precision=highest)  11.1 us
    dot_general x1, matrix products, key_branch(): lax.dot_general(grad_block, weight_block, (((1,), (1,)), ((), ())), prefe...  9.4 us
    broadcast_in_dim x1, other arithmetic, body(): current[None]  6.42 us
  transfers between devices with their start and end apart: 3, of which 2 were waited for; matrix products, arithmetic and copies ran while one was open for 20% of the time, Pallas kernels for 0%

commit v1 on v0

v1 whole, which is shorter than its diff:
```python
import math

import jax
import jax.numpy as jnp
from jax import lax
from jax.sharding import PartitionSpec as P

highest = lax.Precision.HIGHEST


def thirds(x, axis):
    first = lax.reduce_precision(x, 8, 7)
    rest = x - first
    second = lax.reduce_precision(rest, 8, 7)
    third = rest - second
    return jnp.concatenate([first, second, third], axis).astype(jnp.bfloat16)


def fold_rows(x):
    n = x.shape[0] // 3
    return x[:n] + (x[n : 2 * n] + x[2 * n :])


def mm(a, b, ca, cb):
    return lax.dot_general(a, b, (((ca,), (cb,)), ((), ())), preferred_element_type=jnp.float32)


def flip(x, bit):
    n = lax.axis_size("dp")
    return lax.ppermute(x, "dp", [(i, i ^ (1 << bit)) for i in range(n)])


def my_bit(bit):
    return (lax.axis_index("dp") >> bit) & 1


def scatter_half(x, bit):
    n = x.shape[0] // 2
    mine = my_bit(bit)
    keep = lax.dynamic_slice_in_dim(x, mine * n, n, 0)
    send = lax.dynamic_slice_in_dim(x, (1 - mine) * n, n, 0)
    return keep + flip(send, bit)


def gather_half(x, bit):
    other = flip(x, bit)
    return jnp.where(
        my_bit(bit) == 0, jnp.concatenate([x, other], 0), jnp.concatenate([other, x], 0)
    )


def all_sum(x, scatter_bits):
    n = lax.axis_size("dp")
    bits = n.bit_length() - 1
    if n != 1 << bits:
        return lax.psum(x, "dp")
    split = [b for b in scatter_bits if b < bits]
    for b in split:
        x = scatter_half(x, b)
    for b in range(bits):
        if b not in split:
            x = x + flip(x, b)
    for b in reversed(split):
        x = gather_half(x, b)
    return x


def body(saved_input, out_grad, key_weight, layer_gate, q_prev, error_prev):
    inputs = saved_input[0]
    grads = out_grad[0]
    weights = key_weight[0]
    gate_row = layer_gate[0]
    right_prev = q_prev[0]
    error = error_prev[0, 0]
    replicas = lax.axis_size("dp")
    norm_scale = 1.0 / math.sqrt(inputs.shape[0])

    branch = mm(grads, weights, 1, 1)
    current = (gate_row[None, :] * branch).astype(jnp.bfloat16)
    sections = lax.axis_size("section")
    received = lax.ppermute(current, "section", [(i, i - 1) for i in range(1, sections)])

    q_t = thirds(right_prev.T, 0)
    gq = fold_rows(mm(q_t, grads, 1, 1)) * norm_scale
    left = fold_rows(mm(q_t, error, 1, 1) + mm(thirds(gq, 0), inputs, 1, 0))
    p_t = all_sum(left, (0, 1)) * (1.0 / replicas)

    merged = mm(inputs, grads, 0, 0) * norm_scale + error.astype(jnp.float32)

    p3 = thirds(p_t, 0)
    xp = fold_rows(mm(p3, inputs, 1, 1)) * norm_scale
    right = fold_rows(mm(p3, error, 1, 0) + mm(thirds(xp, 0), grads, 1, 0))
    r_t = all_sum(right, (0,)) * (1.0 / replicas)

    gram_matrix = lax.dot_general(p_t, p_t, (((1,), (1,)), ((), ())), precision=highest)
    triangle = jnp.linalg.cholesky(gram_matrix)
    inverse = lax.linalg.triangular_solve(
        triangle, jnp.eye(triangle.shape[0], dtype=jnp.float32), left_side=True, lower=True
    )
    basis_t = jnp.dot(inverse, p_t, precision=highest)
    right_t = jnp.dot(inverse, r_t, precision=highest)

    b3 = thirds(basis_t, 0)
    q3 = thirds(right_t, 0)
    k = basis_t.shape[0]
    left_terms = jnp.concatenate([b3, b3[: 2 * k], b3[:k]], 0)
    right_terms = jnp.concatenate(
        [q3[:k], q3[:k], q3[:k], q3[k : 2 * k], q3[k : 2 * k], q3[2 * k :]], 0
    )
    approx = mm(left_terms, right_terms, 0, 0)
    error_next = (merged - approx).astype(jnp.bfloat16)

    upper = (gate_row[None, :] * (branch + received.astype(jnp.float32))).astype(jnp.bfloat16)
    return (upper[None], basis_t.T[None], right_t.T[None], error_next[None, None])


def solution(mesh):
    return jax.shard_map(
        body,
        mesh=mesh,
        in_specs=(
            P("section", "dp", None),
            P("section", "dp", None),
            P("section", None, None),
            P("section", None),
            P("section", None, None),
            P("section", "dp", None, None),
        ),
        out_specs=(
            P("section", "dp", None),
            P("section", None, None),
            P("section", None, None),
            P("section", "dp", None, None),
        ),
        check_vma=False,
    )
```

time: 277 us -> 119 us (0.43)
  waiting for transfers between devices: 186 us -> 35.6 us
  starting transfers between devices: 1.49 us -> 15.1 us
  between operations: 14.2 us -> 0.96 us
  matrix products: 55.1 us -> 44.3 us
  other arithmetic: 14.6 us -> 19.8 us
  local copies, waits for them, and re-layouts: 5.43 us -> 2.39 us
    psum x2 -> x0, waiting for transfers between devices: 186 us -> none  [the longest x1 96.3 us: body(): p_mean = lax.psum(local_left, 'dp') / replicas]
    ppermute x1 -> x12, waiting for transfers between devices: 0.01 us -> 35.6 us  [the longest x11 24.1 us: flip(): return lax.ppermute(x, 'dp', [(i, i ^ 1 << bit) for i in range(n)])]
    ppermute x1 -> x12, starting transfers between devices: 1.41 us -> 15.1 us  [the longest x11 13.7 us: flip(): return lax.ppermute(x, 'dp', [(i, i ^ 1 << bit) for i in range(n)])]
    dot_general x6 -> x12, matrix products: 53.4 us -> 43.4 us  [the longest x9 39.6 us: mm(): lax.dot_general(a, b, (((ca,), (cb,)), ((), ())), preferred_element_type=...]
    unnamed x14, local copies, waits for them, and re-layouts: 5.36 us -> 0.04 us
    another operation x5 -> x11, other arithmetic: 6.68 us -> 10.3 us  [the longest x3 4.3 us: body(): triangle = jnp.linalg.cholesky(gram_matrix)]
    broadcast_in_dim x2 -> x1, other arithmetic: 7.96 us -> 4.69 us  [body(): upper[None]]
    add x0 -> x10, other arithmetic: none -> 2.88 us  [the longest x3 1.94 us: scatter_half(): return keep + flip(send, bit)]
  transfers between devices with their start and end apart: 3 -> 12, of which waited for: 2 -> 9; matrix products, arithmetic and copies ran while one was open for 20% -> 42% of each run, Pallas kernels for 0% -> 0%
where the time goes in v1:
time: 119 us; the launch traced here: 118 us
  matrix products  44.3 us (37%)
  waiting for transfers between devices  35.6 us (30%)
  other arithmetic  19.8 us (17%)
  starting transfers between devices  15.1 us (13%)
  local copies, waits for them, and re-layouts  2.39 us (2%)
    dot_general x9, matrix products, mm(): lax.dot_general(a, b, (((ca,), (cb,)), ((), ())), preferred_element_type=...  39.6 us
    ppermute x11, waiting for transfers between devices, flip(): return lax.ppermute(x, 'dp', [(i, i ^ 1 << bit) for i in range(n)])  24.1 us
    ppermute x11, starting transfers between devices, flip(): return lax.ppermute(x, 'dp', [(i, i ^ 1 << bit) for i in range(n)])  13.7 us
    ppermute x1, waiting for transfers between devices, body(): lax.ppermute(current, 'section', [(i, i - 1) for i in range(1, sections)])  11.4 us
    broadcast_in_dim x1, other arithmetic, body(): upper[None]  4.69 us
    another operation x3, other arithmetic, body(): triangle = jnp.linalg.cholesky(gram_matrix)  4.3 us
    another operation x2, other arithmetic, body(): lax.linalg.triangular_solve(triangle, jnp.eye(triangle.shape[0], dtype=jn...  3.72 us
  transfers between devices with their start and end apart: 12, of which 9 were waited for; matrix products, arithmetic and copies ran while one was open for 42% of the time, Pallas kernels for 0%

profile of v1, /device:TPU:0, one launch (start us, length us, event | category | flops | bytes accessed | tf_op | source)
XLA Modules:
  0.0 118.2 jit_solution(10523790081629860965)
XLA Ops:
  0.6 0.0 copy-start
  0.6 1.1 reduce-precision_convert_fusion.7
  1.7 1.4 %fusion.15 = f32[96,384]{1,0:T(8,128)S(1)} fusion(bf16[1,384,768]{2,1,0:T(8,128)(2,1)} %param.7, bf16[32,768]{1,0:T(8,128)(2,1)S(1)} %get-tuple-element.12, bf16[32,768]{1,0:T(8,128)(2,1)S(1)} %get-tuple-element.13, bf16[32,768]{1,0:T(8,128)(2,1)S(1)} %get-tuple-element.11), kind=kOutput, calls=%fused_computation.29 | convolution fusion | flops 57065472 | bytes 884736 | tf_op jit(solution)/shard_map/dot_general | solution.py:25
  3.1 4.8 %fusion.2 = f32[96,4096]{1,0:T(8,128)S(1)} fusion(bf16[1,1,4096,768]{3,2,1,0:T(8,128)(2,1)} %param.11, bf16[32,768]{1,0:T(8,128)(2,1)S(1)} %get-tuple-element.12, bf16[32,768]{1,0:T(8,128)(2,1)S(1)} %get-tuple-element.13, bf16[32,768]{1,0:T(8,128)(2,1)S(1)} %get-tuple-element.11), kind=kOutput, calls=%fused_computation.3 | convolution fusion | flops 604422144 | bytes 8011776 | tf_op jit(solution)/shard_map/dot_general | solution.py:25
  7.9 0.0 copy-done
  7.9 0.7 convolution_add_fusion
  8.7 0.0 copy-start.4
  8.7 0.9 fusion.20
  9.6 1.0 constant_dynamic-slice_fusion.2
  10.6 0.6 collective-permute-start.1
  11.1 1.3 %collective-permute-done.1 = f32[16,4096]{1,0:T(8,128)} collective-permute-done((f32[16,4096]{1,0:T(8,128)S(1)}, f32[16,4096]{1,0:T(8,128)}, u32[]{:S(2)}, u32[]{:S(2)}) %collective-permute-start.1) | collective-permute-done | bytes 262176 | tf_op jit(solution)/shard_map/ppermute | solution.py:30
  12.4 1.1 dynamic-slice_add_fusion
  13.5 0.7 constant_dynamic-slice_fusion.1
  14.1 2.9 %collective-permute-start.2 = (f32[8,4096]{1,0:T(8,128)}, f32[8,4096]{1,0:T(8,128)S(1)}, u32[]{:S(2)}, u32[]{:S(2)}) collective-permute-start(f32[8,4096]{1,0:T(8,128)} %constant_dynamic-slice_fusion.1), channel_id=1, source_target_pairs={{0,2},{1,3},{2,0},{3,1},{4,6},{5,7},{6,4},{7,5},{8,10},{9,11},{10,... | collective-permute-start | bytes 393224 | tf_op jit(solution)/shard_map/ppermute | solution.py:30
  17.0 4.0 %collective-permute-done.2 = f32[8,4096]{1,0:T(8,128)S(1)} collective-permute-done((f32[8,4096]{1,0:T(8,128)}, f32[8,4096]{1,0:T(8,128)S(1)}, u32[]{:S(2)}, u32[]{:S(2)}) %collective-permute-start.2) | collective-permute-done | bytes 131104 | tf_op jit(solution)/shard_map/ppermute | solution.py:30
  21.0 1.9 %collective-permute-start.3 = (f32[8,4096]{1,0:T(8,128)S(1)}, f32[8,4096]{1,0:T(8,128)S(1)}, u32[]{:S(2)}, u32[]{:S(2)}) collective-permute-start(f32[8,4096]{1,0:T(8,128)S(1)} %dynamic-slice_add_fusion.1), channel_id=1, source_target_pairs={{0,4},{1,5},{2,6},{3,7},{4,0},{5,1},{6,2},{7,3},{8,12},{9,13},{10,... | collective-permute-start | bytes 393224 | tf_op jit(solution)/shard_map/ppermute | solution.py:30
  22.9 3.2 %collective-permute-done.3 = f32[8,4096]{1,0:T(8,128)S(1)} collective-permute-done((f32[8,4096]{1,0:T(8,128)S(1)}, f32[8,4096]{1,0:T(8,128)S(1)}, u32[]{:S(2)}, u32[]{:S(2)}) %collective-permute-start.3) | collective-permute-done | bytes 131104 | tf_op jit(solution)/shard_map/ppermute | solution.py:30
  26.1 2.9 %collective-permute-start.4 = (f32[8,4096]{1,0:T(8,128)S(1)}, f32[8,4096]{1,0:T(8,128)S(1)}, u32[]{:S(2)}, u32[]{:S(2)}) collective-permute-start(f32[8,4096]{1,0:T(8,128)S(1)} %add.97), channel_id=1, source_target_pairs={{0,8},{1,9},{2,10},{3,11},{4,12},{5,13},{6,14},{7,15},{8,0},{9,1},... | collective-permute-start | bytes 393224 | tf_op jit(solution)/shard_map/ppermute | solution.py:30
  29.0 4.7 %collective-permute-done.4 = f32[8,4096]{1,0:T(8,128)S(1)} collective-permute-done((f32[8,4096]{1,0:T(8,128)S(1)}, f32[8,4096]{1,0:T(8,128)S(1)}, u32[]{:S(2)}, u32[]{:S(2)}) %collective-permute-start.4) | collective-permute-done | bytes 131104 | tf_op jit(solution)/shard_map/ppermute | solution.py:30
  33.7 1.6 %collective-permute-start.5 = (f32[8,4096]{1,0:T(8,128)S(1)}, f32[8,4096]{1,0:T(8,128)}, u32[]{:S(2)}, u32[]{:S(2)}) collective-permute-start(f32[8,4096]{1,0:T(8,128)S(1)} %add.98), channel_id=1, source_target_pairs={{0,2},{1,3},{2,0},{3,1},{4,6},{5,7},{6,4},{7,5},{8,10},{9,11},{10,... | collective-permute-start | bytes 393224 | tf_op jit(solution)/shard_map/ppermute | solution.py:30
  35.3 9.4 %multiply_convert_fusion.1 = (bf16[384,4096]{1,0:T(8,128)(2,1)}, f32[384,4096]{1,0:T(8,128)}) fusion(f32[4096]{0:T(1024)S(1)} %bitcast.68, bf16[1,4096,768]{2,1,0:T(8,128)(2,1)} %param.8, bf16[1,384,768]{2,1,0:T(8,128)(2,1)} %param.7), kind=kOutput, calls=%fused_computation.8 | convolution fusion | flops 2419064832 | bytes 16334848 | tf_op jit(solution)/shard_map/dot_general | solution.py:25
  44.6 1.5 %collective-permute-start = (bf16[384,4096]{1,0:T(8,128)(2,1)}, bf16[384,4096]{1,0:T(8,128)(2,1)}, u32[]{:S(2)}, u32[]{:S(2)}) collective-permute-start(bf16[384,4096]{1,0:T(8,128)(2,1)} %get-tuple-element.18), channel_id=1, source_target_pairs={{16,0},{17,1},{18,2},{19,3},{20,4},{21,5},{22,6},{23,7},{24,8},{25... | collective-permute-start | bytes 9437192 | tf_op jit(solution)/shard_map/ppermute | solution.py:81
  46.1 0.0 collective-permute-done.5
  46.1 1.0 maximum_select_fusion.1
  47.1 0.1 collective-permute-start.6
  47.2 7.4 %fusion.8 = f32[4096,768]{1,0:T(8,128)} fusion(bf16[1,384,4096]{2,1,0:T(8,128)(2,1)S(1)} %copy-done, bf16[1,384,768]{2,1,0:T(8,128)(2,1)} %param.7), kind=kOutput, calls=%fused_computation.12 | convolution fusion | flops 2415919104 | bytes 16318464 | tf_op jit(solution)/shard_map/dot_general | solution.py:25
  54.6 0.0 collective-permute-done.6
  54.6 1.2 reduce-precision_convert_fusion.3
  55.8 1.1 fusion.10
  56.9 0.0 copy-start.2
  56.9 4.0 %fusion = f32[96,768]{1,0:T(8,128)S(1)} fusion(bf16[1,1,4096,768]{3,2,1,0:T(8,128)(2,1)} %param.11, bf16[32,4096]{1,0:T(8,128)(2,1)S(1)} %get-tuple-element.10, bf16[32,4096]{1,0:T(8,128)(2,1)S(1)} %get-tuple-element.9, bf16[32,4096]{1,0:T(8,128)(2,1)S(1)} %get-tuple-element.8), kind=kOutput, calls=%fused_computation.1 | convolution fusion | flops 606339072 | bytes 7372800 | tf_op jit(solution)/shard_map/dot_general | solution.py:25
  60.9 0.0 copy-done.2
  61.0 0.2 convolution_add_fusion.1
  61.2 0.6 constant_dynamic-slice_fusion
  61.9 0.5 collective-permute-start.7
  62.3 2.0 %fusion.69 = f32[32,32]{1,0:T(8,128)S(1)} fusion(f32[16,4096]{1,0:T(8,128)} %collective-permute-done.6, f32[16,4096]{1,0:T(8,128)S(1)} %maximum_select_fusion.1, pred[]{:T(512)S(6)} %eq.8), kind=kOutput, calls=%fused_computation.125 | convolution fusion | flops 50855936 | bytes 528385 | tf_op jit(solution)/shard_map/dot_general | solution.py:95
  64.3 0.1 copy.10
  64.4 0.6 fusion.58
  65.0 3.6 %cholesky.17 = f32[32,32]{1,0:T(8,128)S(1)} custom-call(f32[32,32]{1,0:T(8,128)} %fusion.58), custom_call_target="Cholesky" | custom-call | tf_op jit(solution)/shard_map/jit(cholesky)/cholesky | solution.py:96
  68.7 0.6 compare_reduce_fusion
  69.3 0.7 fusion.55
  70.0 3.1 %custom-call.6 = f32[1,32,32]{1,2,0:T(8,128)} custom-call(f32[1,32,32]{2,1,0:T(8,128)S(1)} %fusion.55), custom_call_target="InvertDiagBlocksLowerTriangular" | custom-call | tf_op jit(solution)/shard_map/triangular_solve | solution.py:97
  73.1 0.9 fusion.56
  74.0 1.6 %constant_dynamic-update-slice_fusion.2 = (bf16[192,4096]{1,0:T(8,128)(2,1)S(1)}, f32[32,4096]{1,0:T(8,128)S(1)}) fusion(f32[32,32]{1,0:T(8,128)S(1)} %fusion.56, f32[16,4096]{1,0:T(8,128)} %collective-permute-done.6, f32[16,4096]{1,0:T(8,128)S(1)} %maximum_select_fusion.1, pred[]{:T(512)S(6)} %eq.8), kind=kOutput, calls=%fused_computation.97 | convolution fusion | flops 51118080 | bytes 1314817 | tf_op jit(solution)/shard_map/dot_general | solution.py:100
  75.6 0.0 copy-start.1
  75.6 0.0 collective-permute-done.7
  75.6 0.9 dynamic-slice_add_fusion.2
  76.5 0.5 collective-permute-start.8
  77.0 0.1 fusion.22
  77.1 3.5 %collective-permute-done.8 = f32[16,768]{1,0:T(8,128)S(1)} collective-permute-done((f32[16,768]{1,0:T(8,128)S(1)}, f32[16,768]{1,0:T(8,128)S(1)}, u32[]{:S(2)}, u32[]{:S(2)}) %collective-permute-start.8) | collective-permute-done | bytes 49184 | tf_op jit(solution)/shard_map/ppermute | solution.py:30
  80.6 0.7 collective-permute-start.9
  81.4 3.4 %collective-permute-done.9 = f32[16,768]{1,0:T(8,128)S(1)} collective-permute-done((f32[16,768]{1,0:T(8,128)S(1)}, f32[16,768]{1,0:T(8,128)S(1)}, u32[]{:S(2)}, u32[]{:S(2)}) %collective-permute-start.9) | collective-permute-done | bytes 49184 | tf_op jit(solution)/shard_map/ppermute | solution.py:30
  84.8 2.1 %collective-permute-start.10 = (f32[16,768]{1,0:T(8,128)S(1)}, f32[16,768]{1,0:T(8,128)S(1)}, u32[]{:S(2)}, u32[]{:S(2)}) collective-permute-start(f32[16,768]{1,0:T(8,128)S(1)} %add.107), channel_id=1, source_target_pairs={{0,8},{1,9},{2,10},{3,11},{4,12},{5,13},{6,14},{7,15},{8,0},{9,1},... | collective-permute-start | bytes 147464 | tf_op jit(solution)/shard_map/ppermute | solution.py:30
  86.9 2.9 %collective-permute-done.10 = f32[16,768]{1,0:T(8,128)S(1)} collective-permute-done((f32[16,768]{1,0:T(8,128)S(1)}, f32[16,768]{1,0:T(8,128)S(1)}, u32[]{:S(2)}, u32[]{:S(2)}) %collective-permute-start.10) | collective-permute-done | bytes 49184 | tf_op jit(solution)/shard_map/ppermute | solution.py:30
  89.8 0.1 collective-permute-start.11
  89.9 1.2 collective-permute-done.11
  91.1 0.2 constant_dynamic-update-slice_fusion.7
  91.3 0.0 copy-start.3
  91.4 0.0 slice-start
  91.5 0.0 slice-start.1
  91.5 10.6 %fusion.6 = bf16[1,1,4096,768]{3,2,1,0:T(8,128)(2,1)} fusion(bf16[192,4096]{1,0:T(8,128)(2,1)S(1)} %constant_dynamic-update-slice_fusion, bf16[192,768]{1,0:T(8,128)(2,1)S(1)} %fusion.46, bf16[1,1,4096,768]{3,2,1,0:T(8,128)(2,1)} %param.11, f32[4096,768]{1,0:T(8,128)} %fusion.8), kind=kOutput, calls=%fused_computation.9 | convolution fusion | flops 1223688192 | bytes 27033600 | tf_op jit(solution)/shard_map/dot_general | solution.py:25
  102.1 0.0 copy-done.3
  102.1 11.4 %collective-permute-done = bf16[384,4096]{1,0:T(8,128)(2,1)} collective-permute-done((bf16[384,4096]{1,0:T(8,128)(2,1)}, bf16[384,4096]{1,0:T(8,128)(2,1)}, u32[]{:S(2)}, u32[]{:S(2)}) %collective-permute-start) | collective-permute-done | bytes 3145760 | tf_op jit(solution)/shard_map/ppermute | solution.py:81
  113.5 4.7 %fusion.7 = bf16[1,384,4096]{2,1,0:T(8,128)(2,1)} fusion(f32[384,4096]{1,0:T(8,128)S(1)} %bitcast.65, bf16[384,4096]{1,0:T(8,128)(2,1)} %collective-permute-done, f32[4096]{0:T(1024)S(1)} %bitcast.69), kind=kLoop, calls=%fused_computation.11 | loop fusion | flops 6291456 | bytes 12599296 | tf_op jit(solution)/shard_map/broadcast_in_dim | solution.py:114
  (26 shorter events, 0.4 us)
Async XLA Ops:
  0.6 7.3 %copy-start = (bf16[1,384,4096]{2,1,0:T(8,128)(2,1)S(1)}, bf16[1,384,4096]{2,1,0:T(8,128)(2,1)}, u32[]{:S(2)}) copy-start(bf16[1,384,4096]{2,1,0:T(8,128)(2,1)} %param.6) | copy-start | bytes 9437188
  8.7 26.6 %copy-start.4 = (f32[1,4096]{1,0:T(1,128)S(1)}, f32[1,4096]{1,0:T(1,128)}, u32[]{:S(2)}) copy-start(f32[1,4096]{1,0:T(1,128)} %param.9) | copy-start | bytes 49156
  10.6 1.9 %collective-permute-start.1 = (f32[16,4096]{1,0:T(8,128)S(1)}, f32[16,4096]{1,0:T(8,128)}, u32[]{:S(2)}, u32[]{:S(2)}) collective-permute-start(f32[16,4096]{1,0:T(8,128)S(1)} %constant_dynamic-slice_fusion.2), channel_id=1, source_target_pairs={{0,1},{1,0},{2,3},{3,2},{4,5},{5,4},{6,7},{7,6},{8,9},{9,8},{10,11... | collective-permute-start | bytes 786440 | tf_op jit(solution)/shard_map/ppermute | solution.py:30
  14.1 6.9 %collective-permute-start.2 = (f32[8,4096]{1,0:T(8,128)}, f32[8,4096]{1,0:T(8,128)S(1)}, u32[]{:S(2)}, u32[]{:S(2)}) collective-permute-start(f32[8,4096]{1,0:T(8,128)} %constant_dynamic-slice_fusion.1), channel_id=1, source_target_pairs={{0,2},{1,3},{2,0},{3,1},{4,6},{5,7},{6,4},{7,5},{8,10},{9,11},{10,... | collective-permute-start | bytes 393224 | tf_op jit(solution)/shard_map/ppermute | solution.py:30
  21.0 5.0 %collective-permute-start.3 = (f32[8,4096]{1,0:T(8,128)S(1)}, f32[8,4096]{1,0:T(8,128)S(1)}, u32[]{:S(2)}, u32[]{:S(2)}) collective-permute-start(f32[8,4096]{1,0:T(8,128)S(1)} %dynamic-slice_add_fusion.1), channel_id=1, source_target_pairs={{0,4},{1,5},{2,6},{3,7},{4,0},{5,1},{6,2},{7,3},{8,12},{9,13},{10,... | collective-permute-start | bytes 393224 | tf_op jit(solution)/shard_map/ppermute | solution.py:30
  26.1 7.6 %collective-permute-start.4 = (f32[8,4096]{1,0:T(8,128)S(1)}, f32[8,4096]{1,0:T(8,128)S(1)}, u32[]{:S(2)}, u32[]{:S(2)}) collective-permute-start(f32[8,4096]{1,0:T(8,128)S(1)} %add.97), channel_id=1, source_target_pairs={{0,8},{1,9},{2,10},{3,11},{4,12},{5,13},{6,14},{7,15},{8,0},{9,1},... | collective-permute-start | bytes 393224 | tf_op jit(solution)/shard_map/ppermute | solution.py:30
  33.7 12.4 %collective-permute-start.5 = (f32[8,4096]{1,0:T(8,128)S(1)}, f32[8,4096]{1,0:T(8,128)}, u32[]{:S(2)}, u32[]{:S(2)}) collective-permute-start(f32[8,4096]{1,0:T(8,128)S(1)} %add.98), channel_id=1, source_target_pairs={{0,2},{1,3},{2,0},{3,1},{4,6},{5,7},{6,4},{7,5},{8,10},{9,11},{10,... | collective-permute-start | bytes 393224 | tf_op jit(solution)/shard_map/ppermute | solution.py:30
  44.6 68.9 %collective-permute-start = (bf16[384,4096]{1,0:T(8,128)(2,1)}, bf16[384,4096]{1,0:T(8,128)(2,1)}, u32[]{:S(2)}, u32[]{:S(2)}) collective-permute-start(bf16[384,4096]{1,0:T(8,128)(2,1)} %get-tuple-element.18), channel_id=1, source_target_pairs={{16,0},{17,1},{18,2},{19,3},{20,4},{21,5},{22,6},{23,7},{24,8},{25... | collective-permute-start | bytes 9437192 | tf_op jit(solution)/shard_map/ppermute | solution.py:81
  47.1 7.5 %collective-permute-start.6 = (f32[16,4096]{1,0:T(8,128)S(1)}, f32[16,4096]{1,0:T(8,128)}, u32[]{:S(2)}, u32[]{:S(2)}) collective-permute-start(f32[16,4096]{1,0:T(8,128)S(1)} %maximum_select_fusion.1), channel_id=1, source_target_pairs={{0,1},{1,0},{2,3},{3,2},{4,5},{5,4},{6,7},{7,6},{8,9},{9,8},{10,11... | collective-permute-start | bytes 786440 | tf_op jit(solution)/shard_map/ppermute | solution.py:30
  56.9 4.1 %copy-start.2 = (bf16[1,384,768]{2,1,0:T(8,128)(2,1)S(1)}, bf16[1,384,768]{2,1,0:T(8,128)(2,1)}, u32[]{:S(2)}) copy-start(bf16[1,384,768]{2,1,0:T(8,128)(2,1)} %param.7) | copy-start | bytes 1769476
  61.9 13.8 %collective-permute-start.7 = (f32[16,768]{1,0:T(8,128)}, f32[16,768]{1,0:T(8,128)}, u32[]{:S(2)}, u32[]{:S(2)}) collective-permute-start(f32[16,768]{1,0:T(8,128)} %constant_dynamic-slice_fusion), channel_id=1, source_target_pairs={{0,1},{1,0},{2,3},{3,2},{4,5},{5,4},{6,7},{7,6},{8,9},{9,8},{10,11... | collective-permute-start | bytes 147464 | tf_op jit(solution)/shard_map/ppermute | solution.py:30
  75.6 26.5 %copy-start.1 = (f32[32,4096]{1,0:T(8,128)}, f32[32,4096]{1,0:T(8,128)S(1)}, u32[]{:S(2)}) copy-start(f32[32,4096]{1,0:T(8,128)S(1)} %get-tuple-element.21) | copy-start | bytes 1572868
  76.5 4.1 %collective-permute-start.8 = (f32[16,768]{1,0:T(8,128)S(1)}, f32[16,768]{1,0:T(8,128)S(1)}, u32[]{:S(2)}, u32[]{:S(2)}) collective-permute-start(f32[16,768]{1,0:T(8,128)S(1)} %dynamic-slice_add_fusion.2), channel_id=1, source_target_pairs={{0,2},{1,3},{2,0},{3,1},{4,6},{5,7},{6,4},{7,5},{8,10},{9,11},{10,... | collective-permute-start | bytes 147464 | tf_op jit(solution)/shard_map/ppermute | solution.py:30
  80.6 4.2 %collective-permute-start.9 = (f32[16,768]{1,0:T(8,128)S(1)}, f32[16,768]{1,0:T(8,128)S(1)}, u32[]{:S(2)}, u32[]{:S(2)}) collective-permute-start(f32[16,768]{1,0:T(8,128)S(1)} %add.106), channel_id=1, source_target_pairs={{0,4},{1,5},{2,6},{3,7},{4,0},{5,1},{6,2},{7,3},{8,12},{9,13},{10,... | collective-permute-start | bytes 147464 | tf_op jit(solution)/shard_map/ppermute | solution.py:30
  84.8 5.0 %collective-permute-start.10 = (f32[16,768]{1,0:T(8,128)S(1)}, f32[16,768]{1,0:T(8,128)S(1)}, u32[]{:S(2)}, u32[]{:S(2)}) collective-permute-start(f32[16,768]{1,0:T(8,128)S(1)} %add.107), channel_id=1, source_target_pairs={{0,8},{1,9},{2,10},{3,11},{4,12},{5,13},{6,14},{7,15},{8,0},{9,1},... | collective-permute-start | bytes 147464 | tf_op jit(solution)/shard_map/ppermute | solution.py:30
  89.8 1.3 %collective-permute-start.11 = (f32[16,768]{1,0:T(8,128)S(1)}, f32[16,768]{1,0:T(8,128)S(1)}, u32[]{:S(2)}, u32[]{:S(2)}) collective-permute-start(f32[16,768]{1,0:T(8,128)S(1)} %add.108), channel_id=1, source_target_pairs={{0,1},{1,0},{2,3},{3,2},{4,5},{5,4},{6,7},{7,6},{8,9},{9,8},{10,11... | collective-permute-start | bytes 147464 | tf_op jit(solution)/shard_map/ppermute | solution.py:30
  91.3 10.7 %copy-start.3 = (f32[32,768]{1,0:T(8,128)}, f32[32,768]{1,0:T(8,128)S(1)}, u32[]{:S(2)}) copy-start(f32[32,768]{1,0:T(8,128)S(1)} %get-tuple-element.23) | copy-start | bytes 294916
  91.4 22.1 %slice-start = ((s8[6291456]{0:T(1024)(128)(4,1)}), s8[4194304]{0:T(1024)(128)(4,1)S(1)}, s32[]{:S(2)}) async-start(s8[6291456]{0:T(1024)(128)(4,1)} %bitcast.64), calls=%async_computation | async-start | bytes 8388608
  91.5 22.1 %slice-start.1 = ((s8[6291456]{0:T(1024)(128)(4,1)}), s8[2097152]{0:T(1024)(128)(4,1)S(1)}, s32[]{:S(2)}) async-start(s8[6291456]{0:T(1024)(128)(4,1)} %bitcast.64), calls=%async_computation.1 | async-start | bytes 4194304

commit v2 on v0

v2 whole, which is shorter than its diff:
```python
import functools
import math

import jax
import jax.numpy as jnp
from jax import lax
from jax.experimental import pallas as pl
from jax.experimental.pallas import tpu as pltpu
from jax.sharding import PartitionSpec as P

highest = lax.Precision.HIGHEST
f32 = jnp.float32
bf16 = jnp.bfloat16


def mm(a, b, ca, cb, precision=None):
    return lax.dot_general(
        a, b, (((ca,), (cb,)), ((), ())), preferred_element_type=f32, precision=precision
    )


def split(x, terms):
    out = []
    for _ in range(terms):
        out.append(x.astype(bf16))
        x = x - out[-1].astype(f32)
    return out


def thirds(x):
    return jnp.concatenate(split(x, 3), 0)


def fold(x):
    n = x.shape[0] // 3
    return x[:n] + (x[n : 2 * n] + x[2 * n :])


def place(me_ref, j, quarter):
    high = (me_ref[0] ^ (j >> 1)) * (2 * quarter)
    low = (me_ref[1] ^ (j & 1)) * quarter
    return pl.multiple_of(high + low, quarter)


def left_kernel(
    me_ref, q_ref, g_ref, x_hbm, e_hbm, keep_ref, send_ref, x_ref, e_ref, x_sem, e_sem, *, scale, steps,
):
    rank = q_ref.shape[0]
    quarter = rank // 4
    width = x_ref.shape[1] // steps
    copies = []
    for i in range(steps):
        at = pl.ds(i * width, width)
        copies.append(
            (
                pltpu.make_async_copy(e_hbm.at[at, :], e_ref.at[at, :], e_sem.at[i]),
                pltpu.make_async_copy(x_hbm.at[:, at], x_ref.at[:, at], x_sem.at[i]),
            )
        )
        for copy in copies[-1]:
            copy.start()
    rows = [q_ref[pl.ds(place(me_ref, j, quarter), quarter), :] for j in range(4)]
    q3 = thirds(jnp.concatenate(rows, 0))
    gq3 = thirds(fold(mm(q3, g_ref[...], 1, 1)) * scale)
    for i in range(steps):
        at = pl.ds(i * width, width)
        for copy in copies[i]:
            copy.wait()
        left = fold(mm(q3, e_ref[at, :], 1, 1) + mm(gq3, x_ref[:, at], 1, 0))
        keep_ref[:, at] = left[: rank // 2]
        send_ref[:, at] = left[rank // 2 :]


def in_order(me_ref, out_ref, pm_ref, py_ref, pc_ref, mean):
    quarter = pm_ref.shape[0]
    parts = [pm_ref[...], py_ref[...], pc_ref[:quarter, :], pc_ref[quarter:, :]]
    for j in range(4):
        out_ref[pl.ds(place(me_ref, j, quarter), quarter), :] = parts[j] * mean


def right_kernel(
    me_ref, pm_ref, py_ref, pc_ref, g_ref, x_ref, e_ref,
    keep_ref, send_ref, gram_ref, ord_ref, acc_ref, *, scale, mean,
):
    rank = ord_ref.shape[0]
    half = rank // 2
    in_order(me_ref, ord_ref, pm_ref, py_ref, pc_ref, mean)
    p3 = thirds(ord_ref[...])
    xp3 = thirds(fold(mm(p3, x_ref[...], 1, 1)) * scale)
    acc_ref[...] = fold(mm(p3, e_ref[...], 1, 0) + mm(xp3, g_ref[...], 1, 0)) * mean
    gram_ref[...] = mm(p3, p3, 1, 1)
    keep_ref[...] = acc_ref[pl.ds(pl.multiple_of(me_ref[0] * half, half), half), :]
    send_ref[...] = acc_ref[pl.ds(pl.multiple_of((1 - me_ref[0]) * half, half), half), :]


def factor_kernel(gram_ref, inv_ref):
    rank = inv_ref.shape[0]
    wide = fold(gram_ref[...])
    a = wide[:, :rank] + (wide[:, rank : 2 * rank] + wide[:, 2 * rank :])
    row = lax.broadcasted_iota(jnp.int32, (rank, rank), 0)
    col = lax.broadcasted_iota(jnp.int32, (rank, rank), 1)
    b = (row == col).astype(f32)
    pivots = jnp.ones((rank, rank), f32)
    for j in range(rank):
        pivot = a[j : j + 1, j : j + 1]
        pivots = jnp.where(row == j, pivot, pivots)
        ratio = jnp.where(row > j, a[:, j : j + 1] / pivot, 0.0)
        b = b - ratio * b[j : j + 1, :]
        a = a - ratio * a[j : j + 1, :]
    inv_ref[...] = b / jnp.sqrt(pivots)


def merged_kernel(x_ref, g_ref, e_ref, out_ref, *, scale, at):
    rows = out_ref.shape[0]
    x = x_ref[:, at : at + rows]
    out_ref[...] = mm(x, g_ref[...], 0, 0) * scale + e_ref[at : at + rows, :].astype(f32)


def basis_kernel(me_ref, inv_ref, pm_ref, py_ref, pc_ref, basis_ref, terms_ref, ord_ref, *, mean):
    in_order(me_ref, ord_ref, pm_ref, py_ref, pc_ref, mean)
    basis_t = mm(inv_ref[...], ord_ref[...], 1, 0, highest)
    basis_ref[...] = basis_t
    hi, lo = split(basis_t, 2)
    terms_ref[...] = jnp.concatenate([hi, lo, hi, jnp.zeros_like(hi)], 0).T


def final_kernel(me_ref, inv_ref, rk_ref, ro_ref, terms_ref, *rest, halves):
    merged_refs = rest[:halves]
    err_ref, q_ref, rt_ref, q3_ref = rest[halves:]
    half = rk_ref.shape[0]
    rows = err_ref.shape[0]

    @pl.when(pl.program_id(0) == 0)
    def _():
        rt_ref[pl.ds(pl.multiple_of(me_ref[0] * half, half), half), :] = rk_ref[...]
        rt_ref[pl.ds(pl.multiple_of((1 - me_ref[0]) * half, half), half), :] = ro_ref[...]
        q_t = mm(inv_ref[...], rt_ref[...], 1, 0, highest)
        q_ref[...] = q_t
        hi, lo = split(q_t, 2)
        q3_ref[...] = jnp.concatenate([hi, hi, lo, jnp.zeros_like(hi)], 0)

    per = merged_refs[0].shape[0] // rows
    i = pl.program_id(0)
    approx = mm(terms_ref[pl.ds(pl.multiple_of(i * rows, rows), rows), :], q3_ref[...], 1, 0)
    for h in range(halves):

        @pl.when(i // per == h)
        def _(h=h):
            at = pl.multiple_of((i - h * per) * rows, rows)
            err_ref[...] = (merged_refs[h][pl.ds(at, rows), :] - approx).astype(bf16)


def branch_kernel(gate_ref, g_ref, w_ref, out_ref):
    out_ref[...] = (gate_ref[...] * mm(g_ref[...], w_ref[...], 1, 1)).astype(bf16)


def upper_kernel(gate_ref, g_ref, w_ref, c_ref, *rest):
    out_ref = rest[-1]
    branch = mm(g_ref[...], w_ref[...], 1, 1)
    out_ref[...] = (gate_ref[...] * (branch + c_ref[...].astype(f32))).astype(bf16)


def whole(shape):
    return pl.BlockSpec(shape, lambda i: (0,) * len(shape))


def down(height, cols):
    return pl.BlockSpec((height, cols), lambda i: (i, 0))


smem = pl.BlockSpec(memory_space=pltpu.SMEM)
near = pl.BlockSpec(memory_space=pltpu.VMEM)
far_off = pl.BlockSpec(memory_space=pltpu.HBM)
plain = pltpu.CompilerParams(vmem_limit_bytes=24 << 20)
order = pltpu.CompilerParams(dimension_semantics=("arbitrary",), vmem_limit_bytes=24 << 20)


def flip(x, bit):
    n = lax.axis_size("dp")
    return lax.ppermute(x, "dp", [(i, i ^ (1 << bit)) for i in range(n)])


def step(saved_input, out_grad, key_weight, layer_gate, q_prev, error_prev):
    inputs = saved_input[0]
    grads = out_grad[0]
    weights = key_weight[0]
    gate_row = layer_gate
    right_prev = q_prev[0]
    error = error_prev[0, 0]
    tokens, wide = inputs.shape
    keys, rank = right_prev.shape
    right_t = right_prev.T
    half, quarter = rank // 2, rank // 4
    replicas = lax.axis_size("dp")
    bits = replicas.bit_length() - 1
    assert replicas == 1 << bits and bits >= 2
    scale = 1.0 / math.sqrt(tokens)
    mean = 1.0 / replicas
    weights = pltpu.with_memory_space_constraint(weights, pltpu.HBM)
    sections = lax.axis_size("section")
    route = [(i, i - 1) for i in range(1, sections)]
    place_in = lax.axis_index("dp")
    me = jnp.stack([place_in & 1, (place_in >> 1) & 1]).astype(jnp.int32)

    unit = wide // 4 if wide % 512 == 0 else wide
    cuts = [(0, 1), (2, 2), (1, 1)] if unit < wide else [(0, 1)]
    received = []
    for at, size in cuts:
        span = size * unit
        current = pl.pallas_call(
            branch_kernel,
            grid=(1,),
            in_specs=[
                pl.BlockSpec((1, span), lambda _, k=at // size: (0, k)),
                whole((tokens, keys)),
                pl.BlockSpec((span, keys), lambda _, k=at // size: (k, 0)),
            ],
            out_specs=whole((tokens, span)),
            out_shape=jax.ShapeDtypeStruct((tokens, span), bf16),
            compiler_params=order,
            name="branch",
        )(gate_row, grads, weights)
        received.append(lax.ppermute(current, "section", route))

    unit_steps = wide // unit
    keep, send, inputs_near, error_near = pl.pallas_call(
        functools.partial(left_kernel, scale=scale, steps=unit_steps),
        in_specs=[smem, near, near, far_off, far_off],
        out_specs=[near] * 4,
        out_shape=[
            pltpu.VMEM((half, wide), f32),
            pltpu.VMEM((half, wide), f32),
            pltpu.VMEM(inputs.shape, bf16),
            pltpu.VMEM(error.shape, bf16),
        ],
        scratch_shapes=[pltpu.SemaphoreType.DMA((unit_steps,)), pltpu.SemaphoreType.DMA((unit_steps,))],
        compiler_params=plain,
        name="left",
    )(me, right_t, grads, inputs, error)

    chip = keep + flip(send, 0)
    mine = chip[:quarter] + flip(chip[quarter:], 1)
    for b in range(2, bits):
        mine = mine + flip(mine, b)
    beside = flip(mine, 1)
    far = flip(jnp.concatenate([mine, beside], 0), 0)

    merged = []
    for h in range(2):
        rows = wide // 2
        merged.append(
            pl.pallas_call(
                functools.partial(merged_kernel, scale=scale, at=h * rows),
                in_specs=[near] * 3,
                out_specs=near,
                out_shape=pltpu.VMEM((rows, keys), f32),
                compiler_params=plain,
                name="merged",
            )(inputs_near, grads, error_near)
        )

    keep, send, gram = pl.pallas_call(
        functools.partial(right_kernel, scale=scale, mean=mean),
        in_specs=[smem] + [near] * 6,
        out_specs=[near] * 3,
        out_shape=[pltpu.VMEM((half, keys), f32)] * 2 + [pltpu.VMEM((3 * rank, 3 * rank), f32)],
        scratch_shapes=[pltpu.VMEM((rank, wide), f32), pltpu.VMEM((rank, keys), f32)],
        compiler_params=plain,
        name="right",
    )(me, mine, beside, far, grads, inputs_near, error_near)

    total = keep + flip(send, 0)
    for b in range(1, bits):
        total = total + flip(total, b)
    other = flip(total, 0)

    inverse = pl.pallas_call(
        factor_kernel,
        out_shape=jax.ShapeDtypeStruct((rank, rank), f32),
        compiler_params=pltpu.CompilerParams(vmem_limit_bytes=4 << 20),
        name="factor",
    )(gram)

    basis_t, terms = pl.pallas_call(
        functools.partial(basis_kernel, mean=mean),
        in_specs=[smem] + [near] * 4,
        out_specs=[near] * 2,
        out_shape=[jax.ShapeDtypeStruct((rank, wide), f32), pltpu.VMEM((wide, 4 * rank), bf16)],
        scratch_shapes=[pltpu.VMEM((rank, wide), f32)],
        compiler_params=plain,
        name="basis",
    )(me, inverse, mine, beside, far)

    error_next, q_t = pl.pallas_call(
        functools.partial(final_kernel, halves=2),
        grid=(unit_steps,),
        in_specs=[smem] + [near] * 6,
        out_specs=[down(unit, keys), whole((rank, keys))],
        out_shape=[
            jax.ShapeDtypeStruct((wide, keys), bf16),
            jax.ShapeDtypeStruct((rank, keys), f32),
        ],
        scratch_shapes=[pltpu.VMEM((rank, keys), f32), pltpu.VMEM((4 * rank, keys), bf16)],
        compiler_params=order,
        name="final",
    )(me, inverse, total, other, terms, *merged)

    upper = None
    for n, (at, size) in enumerate(cuts):
        span = size * unit
        block = pl.BlockSpec((tokens, span), lambda _, k=at // size: (0, k))
        specs = [
            pl.BlockSpec((1, span), lambda _, k=at // size: (0, k)),
            whole((tokens, keys)),
            pl.BlockSpec((span, keys), lambda _, k=at // size: (k, 0)),
            whole((tokens, span)),
        ]
        held = () if upper is None else (upper,)
        upper = pl.pallas_call(
            upper_kernel,
            grid=(1,),
            in_specs=specs + [pl.BlockSpec(memory_space=pl.ANY)] * len(held),
            out_specs=block,
            out_shape=jax.ShapeDtypeStruct((tokens, wide), bf16),
            input_output_aliases={4: 0} if held else {},
            compiler_params=order,
            name="upper",
        )(gate_row, grads, weights, received[n], *held)
    return (upper[None], basis_t.T[None], q_t.T[None], error_next[None, None])


def solution(mesh):
    return spread(mesh)


def spread(mesh):
    return jax.shard_map(
        step,
        mesh=mesh,
        in_specs=(
            P("section", "dp", None),
            P("section", "dp", None),
            P("section", None, None),
            P("section", None),
            P("section", None, None),
            P("section", "dp", None, None),
        ),
        out_specs=(
            P("section", "dp", None),
            P("section", None, None),
            P("section", None, None),
            P("section", "dp", None, None),
        ),
        check_vma=False,
    )
```

time: 277 us -> 100 us (0.36)
  waiting for transfers between devices: 186 us -> 31 us
  matrix products: 55.1 us -> 0 us
  Pallas kernels: 0 us -> 43.9 us
  starting transfers between devices: 1.49 us -> 17.1 us
  other arithmetic: 14.6 us -> 0.2 us
  between operations: 14.2 us -> 0.81 us
    psum x2 -> x0, waiting for transfers between devices: 186 us -> none  [the longest x1 96.3 us: body(): p_mean = lax.psum(local_left, 'dp') / replicas]
    dot_general x6 -> x0, matrix products: 53.4 us -> none  [the longest x1 15.1 us: body(): approx = jnp.dot(basis, right_mean.T, precision=highest)]
    pallas_call x0 -> x13, Pallas kernels: none -> 43.9 us  [the longest x3 10.7 us: step(): pl.pallas_call(upper_kernel, grid=(1,), in_specs=specs + [pl.BlockSpec(me...]
    ppermute x1 -> x14, waiting for transfers between devices: 0.01 us -> 31 us  [the longest x11 21.6 us: flip(): return lax.ppermute(x, 'dp', [(i, i ^ 1 << bit) for i in range(n)])]
    ppermute x1 -> x14, starting transfers between devices: 1.41 us -> 17.1 us  [the longest x11 13 us: flip(): return lax.ppermute(x, 'dp', [(i, i ^ 1 << bit) for i in range(n)])]
    broadcast_in_dim x2 -> x0, other arithmetic: 7.96 us -> none  [the longest x1 6.42 us: body(): current[None]]
    another operation x5 -> x1, other arithmetic: 6.68 us -> 0.08 us  [step(): me = jnp.stack([place_in & 1, place_in >> 1 & 1]).astype(jnp.int32)]
    unnamed x14 -> x12, local copies, waits for them, and re-layouts: 5.36 us -> 6.64 us
  transfers between devices with their start and end apart: 3 -> 14, of which waited for: 2 -> 9; matrix products, arithmetic and copies ran while one was open for 20% -> 0% of each run, Pallas kernels for 0% -> 34%
where the time goes in v2:
time: 100 us; the launch traced here: 99.7 us
  Pallas kernels  43.9 us (44%)
  waiting for transfers between devices  31 us (31%)
  starting transfers between devices  17.1 us (17%)
  local copies, waits for them, and re-layouts  6.65 us (7%)
    ppermute x11, waiting for transfers between devices, flip(): return lax.ppermute(x, 'dp', [(i, i ^ 1 << bit) for i in range(n)])  21.6 us
    ppermute x11, starting transfers between devices, flip(): return lax.ppermute(x, 'dp', [(i, i ^ 1 << bit) for i in range(n)])  13 us
    pallas_call x3, Pallas kernels, step(): pl.pallas_call(upper_kernel, grid=(1,), in_specs=specs + [pl.BlockSpec(me...  10.7 us
    ppermute x3, waiting for transfers between devices, step(): received.append(lax.ppermute(current, 'section', route))  9.48 us
    pallas_call x3, Pallas kernels, step(): pl.pallas_call(branch_kernel, grid=(1,), in_specs=[pl.BlockSpec((1, span)...  7.73 us
    pallas_call x1, Pallas kernels, step(): pl.pallas_call(functools.partial(left_kernel, scale=scale, steps=unit_ste...  6.78 us
    unnamed x12, local copies, waits for them, and re-layouts  6.64 us
    pallas_call x1, Pallas kernels, step(): pl.pallas_call(functools.partial(final_kernel, halves=2), grid=(unit_step...  6.08 us
  transfers between devices with their start and end apart: 14, of which 9 were waited for; matrix products, arithmetic and copies ran while one was open for 0% of the time, Pallas kernels for 34%

profile of v2, /device:TPU:0, one launch (start us, length us, event | category | flops | bytes accessed | tf_op | source)
XLA Modules:
  0.0 99.7 jit_solution(17611516015930776933)
XLA Ops:
  0.6 0.1 pad_add_fusion.me_ref
  0.7 0.0 copy-start
  0.7 1.1 %copy-done = bf16[1,384,768]{2,1,0:T(8,128)(2,1)S(1)} copy-done((bf16[1,384,768]{2,1,0:T(8,128)(2,1)S(1)}, bf16[1,384,768]{2,1,0:T(8,128)(2,1)}, u32[]{:S(2)}) %copy-start) | copy-done | bytes 589848
  1.8 0.0 copy-start.2
  1.8 2.8 %copy-done.2 = bf16[1,1,4096,768]{3,2,1,0:T(8,128)(2,1)S(1)} copy-done((bf16[1,1,4096,768]{3,2,1,0:T(8,128)(2,1)S(1)}, bf16[1,1,4096,768]{3,2,1,0:T(8,128)(2,1)}, u32[]{:S(2)}) %copy-start.2) | copy-done | bytes 6291480
  4.6 0.0 copy-start.3
  4.6 1.9 %copy-done.3 = bf16[1,384,4096]{2,1,0:T(8,128)(2,1)S(1)} copy-done((bf16[1,384,4096]{2,1,0:T(8,128)(2,1)S(1)}, bf16[1,384,4096]{2,1,0:T(8,128)(2,1)}, u32[]{:S(2)}) %copy-start.3) | copy-done | bytes 3145752
  6.5 0.0 copy-start.5
  6.5 0.9 copy-done.5
  7.3 0.0 copy-start.1
  7.3 0.0 copy-start.4
  7.3 6.8 %left.1 = (f32[16,4096]{1,0:T(8,128)S(1)}, f32[16,4096]{1,0:T(8,128)S(1)}, bf16[384,4096]{1,0:T(8,128)(2,1)S(1)}, bf16[4096,768]{1,0:T(8,128)(2,1)S(1)}) custom-call(s32[2]{0:T(128)S(1)} %pad_add_fusion.me_ref, f32[32,768]{1,0:T(8,128)S(1)} %bitcast.29, bf16[384,768]{1,0:T(8,128)(2,1)S(1)} %bitcast.17, bf16[384,4096]{1,0:T(8,128)(2,1)S(1)} %bitcast.28, ...), custom_call_target="tpu_custom_call" | custom-call | tf_op jit(solution)/shard_map/left/pallas_call | solution.py:226
  14.1 0.6 collective-permute-start.3
  14.7 1.2 %collective-permute-done.3 = f32[16,4096]{1,0:T(8,128)S(1)} collective-permute-done((f32[16,4096]{1,0:T(8,128)S(1)}, f32[16,4096]{1,0:T(8,128)S(1)}, u32[]{:S(2)}, u32[]{:S(2)}) %collective-permute-start.3) | collective-permute-done | bytes 262176 | tf_op jit(solution)/shard_map/ppermute | solution.py:180
  15.9 2.9 %collective-permute-start.4 = (f32[8,4096]{1,0:T(8,128)S(1)}, f32[8,4096]{1,0:T(8,128)S(1)}, u32[]{:S(2)}, u32[]{:S(2)}) collective-permute-start(f32[8,4096]{1,0:T(8,128)S(1)} %slice.9), channel_id=1, source_target_pairs={{0,2},{1,3},{2,0},{3,1},{4,6},{5,7},{6,4},{7,5},{8,10},{9,11},{10,... | collective-permute-start | bytes 393224 | tf_op jit(solution)/shard_map/ppermute | solution.py:180
  18.9 0.0 copy-done.1
  18.9 0.0 copy-done.4
  18.9 3.3 %branch.4 = bf16[384,2048]{1,0:T(8,128)(2,1)S(1)} custom-call(f32[1,4096]{1,0:T(1,128)S(1)} %copy-done.4, bf16[384,768]{1,0:T(8,128)(2,1)S(1)} %bitcast.18, bf16[4096,768]{1,0:T(8,128)(2,1)} %bitcast.30), custom_call_target="tpu_custom_call" | custom-call | tf_op jit(solution)/shard_map/branch/pallas_call | solution.py:210
  22.2 1.3 %collective-permute-start.1 = (bf16[384,2048]{1,0:T(8,128)(2,1)S(1)}, bf16[384,2048]{1,0:T(8,128)(2,1)S(1)}, u32[]{:S(2)}, u32[]{:S(2)}) collective-permute-start(bf16[384,2048]{1,0:T(8,128)(2,1)S(1)} %branch.4), channel_id=1, source_target_pairs={{16,0},{17,1},{18,2},{19,3},{20,4},{21,5},{22,6},{23,7},{24,8},{25... | collective-permute-start | bytes 4718600 | tf_op jit(solution)/shard_map/ppermute | solution.py:223
  23.5 0.0 collective-permute-done.4
  23.5 1.6 %collective-permute-start.5 = (f32[8,4096]{1,0:T(8,128)S(1)}, f32[8,4096]{1,0:T(8,128)S(1)}, u32[]{:S(2)}, u32[]{:S(2)}) collective-permute-start(f32[8,4096]{1,0:T(8,128)S(1)} %slice_add_fusion), channel_id=1, source_target_pairs={{0,4},{1,5},{2,6},{3,7},{4,0},{5,1},{6,2},{7,3},{8,12},{9,13},{10,... | collective-permute-start | bytes 393224 | tf_op jit(solution)/shard_map/ppermute | solution.py:180
  25.2 3.7 %collective-permute-done.5 = f32[8,4096]{1,0:T(8,128)S(1)} collective-permute-done((f32[8,4096]{1,0:T(8,128)S(1)}, f32[8,4096]{1,0:T(8,128)S(1)}, u32[]{:S(2)}, u32[]{:S(2)}) %collective-permute-start.5) | collective-permute-done | bytes 131104 | tf_op jit(solution)/shard_map/ppermute | solution.py:180
  28.9 2.6 %collective-permute-start.6 = (f32[8,4096]{1,0:T(8,128)S(1)}, f32[8,4096]{1,0:T(8,128)S(1)}, u32[]{:S(2)}, u32[]{:S(2)}) collective-permute-start(f32[8,4096]{1,0:T(8,128)S(1)} %add.26), channel_id=1, source_target_pairs={{0,8},{1,9},{2,10},{3,11},{4,12},{5,13},{6,14},{7,15},{8,0},{9,1},... | collective-permute-start | bytes 393224 | tf_op jit(solution)/shard_map/ppermute | solution.py:180
  31.5 5.5 %collective-permute-done.6 = f32[8,4096]{1,0:T(8,128)S(1)} collective-permute-done((f32[8,4096]{1,0:T(8,128)S(1)}, f32[8,4096]{1,0:T(8,128)S(1)}, u32[]{:S(2)}, u32[]{:S(2)}) %collective-permute-start.6) | collective-permute-done | bytes 131104 | tf_op jit(solution)/shard_map/ppermute | solution.py:180
  37.1 0.1 collective-permute-start.7
  37.2 2.2 %branch.5 = bf16[384,1024]{1,0:T(8,128)(2,1)S(1)} custom-call(f32[1,4096]{1,0:T(1,128)S(1)} %copy-done.4, bf16[384,768]{1,0:T(8,128)(2,1)S(1)} %bitcast.19, bf16[4096,768]{1,0:T(8,128)(2,1)} %bitcast.31), custom_call_target="tpu_custom_call" | custom-call | tf_op jit(solution)/shard_map/branch/pallas_call | solution.py:210
  39.4 1.3 %collective-permute-start.2 = (bf16[384,1024]{1,0:T(8,128)(2,1)S(1)}, bf16[384,1024]{1,0:T(8,128)(2,1)S(1)}, u32[]{:S(2)}, u32[]{:S(2)}) collective-permute-start(bf16[384,1024]{1,0:T(8,128)(2,1)S(1)} %branch.5), channel_id=1, source_target_pairs={{16,0},{17,1},{18,2},{19,3},{20,4},{21,5},{22,6},{23,7},{24,8},{25... | collective-permute-start | bytes 2359304 | tf_op jit(solution)/shard_map/ppermute | solution.py:223
  40.7 2.2 %branch.3 = bf16[384,1024]{1,0:T(8,128)(2,1)S(1)} custom-call(f32[1,4096]{1,0:T(1,128)S(1)} %copy-done.4, bf16[384,768]{1,0:T(8,128)(2,1)S(1)} %bitcast.20, bf16[4096,768]{1,0:T(8,128)(2,1)} %bitcast.32), custom_call_target="tpu_custom_call" | custom-call | tf_op jit(solution)/shard_map/branch/pallas_call | solution.py:210
  42.9 1.5 %collective-permute-start = (bf16[384,1024]{1,0:T(8,128)(2,1)S(1)}, bf16[384,1024]{1,0:T(8,128)(2,1)S(1)}, u32[]{:S(2)}, u32[]{:S(2)}) collective-permute-start(bf16[384,1024]{1,0:T(8,128)(2,1)S(1)} %branch.3), channel_id=1, source_target_pairs={{16,0},{17,1},{18,2},{19,3},{20,4},{21,5},{22,6},{23,7},{24,8},{25... | collective-permute-start | bytes 2359304 | tf_op jit(solution)/shard_map/ppermute | solution.py:223
  44.4 0.0 collective-permute-done.7.py_ref
  44.4 0.1 collective-permute-start.8
  44.5 1.5 %collective-permute-done.8.pc_ref = f32[16,4096]{1,0:T(8,128)S(1)} collective-permute-done((f32[16,4096]{1,0:T(8,128)S(1)}, f32[16,4096]{1,0:T(8,128)S(1)}, u32[]{:S(2)}, u32[]{:S(2)}) %collective-permute-start.8) | collective-permute-done | bytes 262176 | tf_op jit(solution)/shard_map/ppermute | solution.py:180
  46.0 4.1 %right.1 = (f32[16,768]{1,0:T(8,128)S(1)}, f32[16,768]{1,0:T(8,128)S(1)}, f32[96,96]{1,0:T(8,128)S(1)}) custom-call(s32[2]{0:T(128)S(1)} %pad_add_fusion.me_ref, f32[8,4096]{1,0:T(8,128)S(1)} %add.27.pm_ref, f32[8,4096]{1,0:T(8,128)S(1)} %collective-permute-done.7.py_ref, f32[16,4096]{1,0:T(8,128)S(1)} %collective-permute-done.8.pc_ref, ...), custom_call_target="tpu_custom_call" | custom-call | tf_op jit(solution)/shard_map/right/pallas_call | solution.py:262
  50.2 0.2 collective-permute-start.9
  50.4 1.1 %collective-permute-done.9 = f32[16,768]{1,0:T(8,128)S(1)} collective-permute-done((f32[16,768]{1,0:T(8,128)S(1)}, f32[16,768]{1,0:T(8,128)S(1)}, u32[]{:S(2)}, u32[]{:S(2)}) %collective-permute-start.9) | collective-permute-done | bytes 49184 | tf_op jit(solution)/shard_map/ppermute | solution.py:180
  51.5 2.0 %collective-permute-start.10 = (f32[16,768]{1,0:T(8,128)S(1)}, f32[16,768]{1,0:T(8,128)S(1)}, u32[]{:S(2)}, u32[]{:S(2)}) collective-permute-start(f32[16,768]{1,0:T(8,128)S(1)} %add.28), channel_id=1, source_target_pairs={{0,2},{1,3},{2,0},{3,1},{4,6},{5,7},{6,4},{7,5},{8,10},{9,11},{10,... | collective-permute-start | bytes 147464 | tf_op jit(solution)/shard_map/ppermute | solution.py:180
  53.5 2.1 %collective-permute-done.10 = f32[16,768]{1,0:T(8,128)S(1)} collective-permute-done((f32[16,768]{1,0:T(8,128)S(1)}, f32[16,768]{1,0:T(8,128)S(1)}, u32[]{:S(2)}, u32[]{:S(2)}) %collective-permute-start.10) | collective-permute-done | bytes 49184 | tf_op jit(solution)/shard_map/ppermute | solution.py:180
  55.6 0.7 collective-permute-start.11
  56.3 3.5 %collective-permute-done.11 = f32[16,768]{1,0:T(8,128)S(1)} collective-permute-done((f32[16,768]{1,0:T(8,128)S(1)}, f32[16,768]{1,0:T(8,128)S(1)}, u32[]{:S(2)}, u32[]{:S(2)}) %collective-permute-start.11) | collective-permute-done | bytes 49184 | tf_op jit(solution)/shard_map/ppermute | solution.py:180
  59.8 2.1 %collective-permute-start.12 = (f32[16,768]{1,0:T(8,128)S(1)}, f32[16,768]{1,0:T(8,128)S(1)}, u32[]{:S(2)}, u32[]{:S(2)}) collective-permute-start(f32[16,768]{1,0:T(8,128)S(1)} %add.30), channel_id=1, source_target_pairs={{0,8},{1,9},{2,10},{3,11},{4,12},{5,13},{6,14},{7,15},{8,0},{9,1},... | collective-permute-start | bytes 147464 | tf_op jit(solution)/shard_map/ppermute | solution.py:180
  61.8 3.0 %collective-permute-done.12 = f32[16,768]{1,0:T(8,128)S(1)} collective-permute-done((f32[16,768]{1,0:T(8,128)S(1)}, f32[16,768]{1,0:T(8,128)S(1)}, u32[]{:S(2)}, u32[]{:S(2)}) %collective-permute-start.12) | collective-permute-done | bytes 49184 | tf_op jit(solution)/shard_map/ppermute | solution.py:180
  64.8 0.1 collective-permute-start.13
  64.9 1.9 %merged.2.rest_0_ = f32[2048,768]{1,0:T(8,128)S(1)} custom-call(bf16[384,4096]{1,0:T(8,128)(2,1)S(1)} %get-tuple-element.17.x_ref, bf16[384,768]{1,0:T(8,128)(2,1)S(1)} %bitcast.22, bf16[4096,768]{1,0:T(8,128)(2,1)S(1)} %get-tuple-element.18.e_ref), custom_call_target="tpu_custom_call" | custom-call | tf_op jit(solution)/shard_map/merged/pallas_call | solution.py:252
  66.8 1.9 %merged.3.rest_1_ = f32[2048,768]{1,0:T(8,128)S(1)} custom-call(bf16[384,4096]{1,0:T(8,128)(2,1)S(1)} %get-tuple-element.17.x_ref, bf16[384,768]{1,0:T(8,128)(2,1)S(1)} %bitcast.23, bf16[4096,768]{1,0:T(8,128)(2,1)S(1)} %get-tuple-element.18.e_ref), custom_call_target="tpu_custom_call" | custom-call | tf_op jit(solution)/shard_map/merged/pallas_call | solution.py:252
  68.7 9.5 %collective-permute-done.2.c_ref = bf16[384,1024]{1,0:T(8,128)(2,1)S(1)} collective-permute-done((bf16[384,1024]{1,0:T(8,128)(2,1)S(1)}, bf16[384,1024]{1,0:T(8,128)(2,1)S(1)}, u32[]{:S(2)}, u32[]{:S(2)}) %collective-permute-start.2) | collective-permute-done | bytes 786464 | tf_op jit(solution)/shard_map/ppermute | solution.py:223
  78.2 3.1 %upper.3.rest_0_ = bf16[384,4096]{1,0:T(8,128)(2,1)} custom-call(f32[1,4096]{1,0:T(1,128)S(1)} %copy-done.4, bf16[384,768]{1,0:T(8,128)(2,1)S(1)} %bitcast.24, bf16[4096,768]{1,0:T(8,128)(2,1)} %bitcast.33, bf16[384,1024]{1,0:T(8,128)(2,1)S(1)} %collective-permute-done.2.c_ref), custom_call_target="tpu_custom_call" | custom-call | tf_op jit(solution)/shard_map/upper/pallas_call | solution.py:319
  81.3 2.8 %factor.1.inv_ref = f32[32,32]{1,0:T(8,128)S(1)} custom-call(f32[96,96]{1,0:T(8,128)S(1)} %get-tuple-element.19.gram_ref), custom_call_target="tpu_custom_call" | custom-call | tf_op jit(solution)/shard_map/factor/pallas_call | solution.py:277
  84.1 1.9 %basis.1 = (f32[32,4096]{1,0:T(8,128)}, bf16[4096,128]{1,0:T(8,128)(2,1)S(1)}) custom-call(s32[2]{0:T(128)S(1)} %pad_add_fusion.me_ref, f32[32,32]{1,0:T(8,128)S(1)} %factor.1.inv_ref, f32[8,4096]{1,0:T(8,128)S(1)} %add.27.pm_ref, f32[8,4096]{1,0:T(8,128)S(1)} %collective-permute-done.7.py_ref, f32[16,4096]{1,0:T(8,128)S(1)} %collective-permute-done.8.pc_ref), custom_call_target="tpu_custom_call" | custom-call | tf_op jit(solution)/shard_map/basis/pallas_call | solution.py:284
  86.0 0.0 collective-permute-done.13.ro_ref
  86.0 6.1 %final.1 = (bf16[4096,768]{1,0:T(8,128)(2,1)}, f32[32,768]{1,0:T(8,128)}) custom-call(s32[2]{0:T(128)S(1)} %pad_add_fusion.me_ref, f32[32,32]{1,0:T(8,128)S(1)} %factor.1.inv_ref, f32[16,768]{1,0:T(8,128)S(1)} %add.31.rk_ref, f32[16,768]{1,0:T(8,128)S(1)} %collective-permute-done.13.ro_ref, bf16[4096,128]{1,0:T(8,128)(2,1)S(1)} %get-tuple-element.23.terms_ref, ...), custom_call_target="tpu_custom_call" | custom-call | tf_op jit(solution)/shard_map/final/pallas_call | solution.py:294
  92.1 0.0 collective-permute-done.1.c_ref
  92.1 4.5 %upper.4.rest_0_ = bf16[384,4096]{1,0:T(8,128)(2,1)} custom-call(f32[1,4096]{1,0:T(1,128)S(1)} %copy-done.4, bf16[384,768]{1,0:T(8,128)(2,1)S(1)} %bitcast.25, bf16[4096,768]{1,0:T(8,128)(2,1)} %bitcast.34, bf16[384,2048]{1,0:T(8,128)(2,1)S(1)} %collective-permute-done.1.c_ref, bf16[384,4096]{1,0:T(8,128)(2,1)} %upper.3.rest_0_), custom_call_target="tpu_custom_call", output_to_operand_aliasing={{}: (4, {})} | custom-call | tf_op jit(solution)/shard_map/upper/pallas_call | solution.py:319
  96.6 0.0 collective-permute-done.c_ref
  96.6 3.1 %upper.5 = bf16[384,4096]{1,0:T(8,128)(2,1)} custom-call(f32[1,4096]{1,0:T(1,128)S(1)} %copy-done.4, bf16[384,768]{1,0:T(8,128)(2,1)S(1)} %bitcast.26, bf16[4096,768]{1,0:T(8,128)(2,1)} %bitcast.35, bf16[384,1024]{1,0:T(8,128)(2,1)S(1)} %collective-permute-done.c_ref, bf16[384,4096]{1,0:T(8,128)(2,1)} %upper.4.rest_0_), custom_call_target="tpu_custom_call", output_to_operand_aliasing={{}: (4, {})} | custom-call | tf_op jit(solution)/shard_map/upper/pallas_call | solution.py:319
  (10 shorter events, 0.1 us)
Async XLA Ops:
  0.7 1.1 %copy-start = (bf16[1,384,768]{2,1,0:T(8,128)(2,1)S(1)}, bf16[1,384,768]{2,1,0:T(8,128)(2,1)}, u32[]{:S(2)}) copy-start(bf16[1,384,768]{2,1,0:T(8,128)(2,1)} %param.7) | copy-start | bytes 1769476
  1.8 2.8 %copy-start.2 = (bf16[1,1,4096,768]{3,2,1,0:T(8,128)(2,1)S(1)}, bf16[1,1,4096,768]{3,2,1,0:T(8,128)(2,1)}, u32[]{:S(2)}) copy-start(bf16[1,1,4096,768]{3,2,1,0:T(8,128)(2,1)} %param.11) | copy-start | bytes 18874372
  4.6 1.9 %copy-start.3 = (bf16[1,384,4096]{2,1,0:T(8,128)(2,1)S(1)}, bf16[1,384,4096]{2,1,0:T(8,128)(2,1)}, u32[]{:S(2)}) copy-start(bf16[1,384,4096]{2,1,0:T(8,128)(2,1)} %param.6) | copy-start | bytes 9437188
  6.5 0.9 copy-start.5
  7.3 11.5 %copy-start.1 = (bf16[1,384,768]{2,1,0:T(8,128)(2,1)S(1)}, bf16[1,384,768]{2,1,0:T(8,128)(2,1)}, u32[]{:S(2)}) copy-start(bf16[1,384,768]{2,1,0:T(8,128)(2,1)} %param.7) | copy-start | bytes 1769476
  7.3 11.5 %copy-start.4 = (f32[1,4096]{1,0:T(1,128)S(1)}, f32[1,4096]{1,0:T(1,128)}, u32[]{:S(2)}) copy-start(f32[1,4096]{1,0:T(1,128)} %gate_ref.11) | copy-start | bytes 49156
  14.1 1.7 %collective-permute-start.3 = (f32[16,4096]{1,0:T(8,128)S(1)}, f32[16,4096]{1,0:T(8,128)S(1)}, u32[]{:S(2)}, u32[]{:S(2)}) collective-permute-start(f32[16,4096]{1,0:T(8,128)S(1)} %get-tuple-element.16), channel_id=1, source_target_pairs={{0,1},{1,0},{2,3},{3,2},{4,5},{5,4},{6,7},{7,6},{8,9},{9,8},{10,11... | collective-permute-start | bytes 786440 | tf_op jit(solution)/shard_map/ppermute | solution.py:180
  15.9 7.6 %collective-permute-start.4 = (f32[8,4096]{1,0:T(8,128)S(1)}, f32[8,4096]{1,0:T(8,128)S(1)}, u32[]{:S(2)}, u32[]{:S(2)}) collective-permute-start(f32[8,4096]{1,0:T(8,128)S(1)} %slice.9), channel_id=1, source_target_pairs={{0,2},{1,3},{2,0},{3,1},{4,6},{5,7},{6,4},{7,5},{8,10},{9,11},{10,... | collective-permute-start | bytes 393224 | tf_op jit(solution)/shard_map/ppermute | solution.py:180
  22.2 69.9 %collective-permute-start.1 = (bf16[384,2048]{1,0:T(8,128)(2,1)S(1)}, bf16[384,2048]{1,0:T(8,128)(2,1)S(1)}, u32[]{:S(2)}, u32[]{:S(2)}) collective-permute-start(bf16[384,2048]{1,0:T(8,128)(2,1)S(1)} %branch.4), channel_id=1, source_target_pairs={{16,0},{17,1},{18,2},{19,3},{20,4},{21,5},{22,6},{23,7},{24,8},{25... | collective-permute-start | bytes 4718600 | tf_op jit(solution)/shard_map/ppermute | solution.py:223
  23.5 5.3 %collective-permute-start.5 = (f32[8,4096]{1,0:T(8,128)S(1)}, f32[8,4096]{1,0:T(8,128)S(1)}, u32[]{:S(2)}, u32[]{:S(2)}) collective-permute-start(f32[8,4096]{1,0:T(8,128)S(1)} %slice_add_fusion), channel_id=1, source_target_pairs={{0,4},{1,5},{2,6},{3,7},{4,0},{5,1},{6,2},{7,3},{8,12},{9,13},{10,... | collective-permute-start | bytes 393224 | tf_op jit(solution)/shard_map/ppermute | solution.py:180
  28.9 8.2 %collective-permute-start.6 = (f32[8,4096]{1,0:T(8,128)S(1)}, f32[8,4096]{1,0:T(8,128)S(1)}, u32[]{:S(2)}, u32[]{:S(2)}) collective-permute-start(f32[8,4096]{1,0:T(8,128)S(1)} %add.26), channel_id=1, source_target_pairs={{0,8},{1,9},{2,10},{3,11},{4,12},{5,13},{6,14},{7,15},{8,0},{9,1},... | collective-permute-start | bytes 393224 | tf_op jit(solution)/shard_map/ppermute | solution.py:180
  37.1 7.3 %collective-permute-start.7 = (f32[8,4096]{1,0:T(8,128)S(1)}, f32[8,4096]{1,0:T(8,128)S(1)}, u32[]{:S(2)}, u32[]{:S(2)}) collective-permute-start(f32[8,4096]{1,0:T(8,128)S(1)} %add.27.pm_ref), channel_id=1, source_target_pairs={{0,2},{1,3},{2,0},{3,1},{4,6},{5,7},{6,4},{7,5},{8,10},{9,11},{10,... | collective-permute-start | bytes 393224 | tf_op jit(solution)/shard_map/ppermute | solution.py:180
  39.4 38.8 %collective-permute-start.2 = (bf16[384,1024]{1,0:T(8,128)(2,1)S(1)}, bf16[384,1024]{1,0:T(8,128)(2,1)S(1)}, u32[]{:S(2)}, u32[]{:S(2)}) collective-permute-start(bf16[384,1024]{1,0:T(8,128)(2,1)S(1)} %branch.5), channel_id=1, source_target_pairs={{16,0},{17,1},{18,2},{19,3},{20,4},{21,5},{22,6},{23,7},{24,8},{25... | collective-permute-start | bytes 2359304 | tf_op jit(solution)/shard_map/ppermute | solution.py:223
  42.9 53.7 %collective-permute-start = (bf16[384,1024]{1,0:T(8,128)(2,1)S(1)}, bf16[384,1024]{1,0:T(8,128)(2,1)S(1)}, u32[]{:S(2)}, u32[]{:S(2)}) collective-permute-start(bf16[384,1024]{1,0:T(8,128)(2,1)S(1)} %branch.3), channel_id=1, source_target_pairs={{16,0},{17,1},{18,2},{19,3},{20,4},{21,5},{22,6},{23,7},{24,8},{25... | collective-permute-start | bytes 2359304 | tf_op jit(solution)/shard_map/ppermute | solution.py:223
  44.4 1.6 %collective-permute-start.8 = (f32[16,4096]{1,0:T(8,128)S(1)}, f32[16,4096]{1,0:T(8,128)S(1)}, u32[]{:S(2)}, u32[]{:S(2)}) collective-permute-start(f32[16,4096]{1,0:T(8,128)S(1)} %pad_maximum_fusion), channel_id=1, source_target_pairs={{0,1},{1,0},{2,3},{3,2},{4,5},{5,4},{6,7},{7,6},{8,9},{9,8},{10,11... | collective-permute-start | bytes 786440 | tf_op jit(solution)/shard_map/ppermute | solution.py:180
  50.2 1.3 %collective-permute-start.9 = (f32[16,768]{1,0:T(8,128)S(1)}, f32[16,768]{1,0:T(8,128)S(1)}, u32[]{:S(2)}, u32[]{:S(2)}) collective-permute-start(f32[16,768]{1,0:T(8,128)S(1)} %get-tuple-element.22), channel_id=1, source_target_pairs={{0,1},{1,0},{2,3},{3,2},{4,5},{5,4},{6,7},{7,6},{8,9},{9,8},{10,11... | collective-permute-start | bytes 147464 | tf_op jit(solution)/shard_map/ppermute | solution.py:180
  51.5 4.1 %collective-permute-start.10 = (f32[16,768]{1,0:T(8,128)S(1)}, f32[16,768]{1,0:T(8,128)S(1)}, u32[]{:S(2)}, u32[]{:S(2)}) collective-permute-start(f32[16,768]{1,0:T(8,128)S(1)} %add.28), channel_id=1, source_target_pairs={{0,2},{1,3},{2,0},{3,1},{4,6},{5,7},{6,4},{7,5},{8,10},{9,11},{10,... | collective-permute-start | bytes 147464 | tf_op jit(solution)/shard_map/ppermute | solution.py:180
  55.6 4.2 %collective-permute-start.11 = (f32[16,768]{1,0:T(8,128)S(1)}, f32[16,768]{1,0:T(8,128)S(1)}, u32[]{:S(2)}, u32[]{:S(2)}) collective-permute-start(f32[16,768]{1,0:T(8,128)S(1)} %add.29), channel_id=1, source_target_pairs={{0,4},{1,5},{2,6},{3,7},{4,0},{5,1},{6,2},{7,3},{8,12},{9,13},{10,... | collective-permute-start | bytes 147464 | tf_op jit(solution)/shard_map/ppermute | solution.py:180
  59.8 5.0 %collective-permute-start.12 = (f32[16,768]{1,0:T(8,128)S(1)}, f32[16,768]{1,0:T(8,128)S(1)}, u32[]{:S(2)}, u32[]{:S(2)}) collective-permute-start(f32[16,768]{1,0:T(8,128)S(1)} %add.30), channel_id=1, source_target_pairs={{0,8},{1,9},{2,10},{3,11},{4,12},{5,13},{6,14},{7,15},{8,0},{9,1},... | collective-permute-start | bytes 147464 | tf_op jit(solution)/shard_map/ppermute | solution.py:180
  64.8 21.2 %collective-permute-start.13 = (f32[16,768]{1,0:T(8,128)S(1)}, f32[16,768]{1,0:T(8,128)S(1)}, u32[]{:S(2)}, u32[]{:S(2)}) collective-permute-start(f32[16,768]{1,0:T(8,128)S(1)} %add.31.rk_ref), channel_id=1, source_target_pairs={{0,1},{1,0},{2,3},{3,2},{4,5},{5,4},{6,7},{7,6},{8,9},{9,8},{10,11... | collective-permute-start | bytes 147464 | tf_op jit(solution)/shard_map/ppermute | solution.py:180

commit v3 on v2

--- a/solution.py
+++ b/solution.py
@@ -150,14 +150,14 @@
             err_ref[...] = (merged_refs[h][pl.ds(at, rows), :] - approx).astype(bf16)
 
 
-def branch_kernel(gate_ref, g_ref, w_ref, out_ref):
-    out_ref[...] = (gate_ref[...] * mm(g_ref[...], w_ref[...], 1, 1)).astype(bf16)
-
-
-def upper_kernel(gate_ref, g_ref, w_ref, c_ref, *rest):
-    out_ref = rest[-1]
+def branch_kernel(gate_ref, g_ref, w_ref, c_ref, branch_ref):
     branch = mm(g_ref[...], w_ref[...], 1, 1)
-    out_ref[...] = (gate_ref[...] * (branch + c_ref[...].astype(f32))).astype(bf16)
+    branch_ref[...] = branch
+    c_ref[...] = (gate_ref[...] * branch).astype(bf16)
+
+
+def upper_kernel(gate_ref, branch_ref, c_ref, *rest):
+    rest[-1][...] = (gate_ref[...] * (branch_ref[...] + c_ref[...].astype(f32))).astype(bf16)
 
 
 def whole(shape):
@@ -196,18 +196,23 @@
     assert replicas == 1 << bits and bits >= 2
     scale = 1.0 / math.sqrt(tokens)
     mean = 1.0 / replicas
-    weights = pltpu.with_memory_space_constraint(weights, pltpu.HBM)
+    weights, inputs, error, grads_far, gate_far = [
+        pltpu.with_memory_space_constraint(a, pltpu.HBM)
+        for a in (weights, inputs, error, grads, gate_row)
+    ]
     sections = lax.axis_size("section")
     route = [(i, i - 1) for i in range(1, sections)]
     place_in = lax.axis_index("dp")
     me = jnp.stack([place_in & 1, (place_in >> 1) & 1]).astype(jnp.int32)
 
     unit = wide // 4 if wide % 512 == 0 else wide
-    cuts = [(0, 1), (2, 2), (1, 1)] if unit < wide else [(0, 1)]
+    part = wide // 8 if wide % 1024 == 0 else wide
+    cuts = [(0, 1), (1, 1), (4, 4), (2, 2)] if part < wide else [(0, 1)]
+    branches = []
     received = []
     for at, size in cuts:
-        span = size * unit
-        current = pl.pallas_call(
+        span = size * part
+        current, branch = pl.pallas_call(
             branch_kernel,
             grid=(1,),
             in_specs=[
@@ -215,16 +220,18 @@
                 whole((tokens, keys)),
                 pl.BlockSpec((span, keys), lambda _, k=at // size: (k, 0)),
             ],
-            out_specs=whole((tokens, span)),
-            out_shape=jax.ShapeDtypeStruct((tokens, span), bf16),
+            out_specs=[whole((tokens, span)), near],
+            out_shape=[jax.ShapeDtypeStruct((tokens, span), bf16), pltpu.VMEM((tokens, span), f32)],
             compiler_params=order,
             name="branch",
-        )(gate_row, grads, weights)
+        )(gate_far, grads_far, weights)
+        branches.append(branch)
         received.append(lax.ppermute(current, "section", route))
 
     unit_steps = wide // unit
+    left_steps = wide // part
     keep, send, inputs_near, error_near = pl.pallas_call(
-        functools.partial(left_kernel, scale=scale, steps=unit_steps),
+        functools.partial(left_kernel, scale=scale, steps=left_steps),
         in_specs=[smem, near, near, far_off, far_off],
         out_specs=[near] * 4,
         out_shape=[
@@ -233,7 +240,7 @@
             pltpu.VMEM(inputs.shape, bf16),
             pltpu.VMEM(error.shape, bf16),
         ],
-        scratch_shapes=[pltpu.SemaphoreType.DMA((unit_steps,)), pltpu.SemaphoreType.DMA((unit_steps,))],
+        scratch_shapes=[pltpu.SemaphoreType.DMA((left_steps,)), pltpu.SemaphoreType.DMA((left_steps,))],
         compiler_params=plain,
         name="left",
     )(me, right_t, grads, inputs, error)
@@ -307,12 +314,11 @@
 
     upper = None
     for n, (at, size) in enumerate(cuts):
-        span = size * unit
+        span = size * part
         block = pl.BlockSpec((tokens, span), lambda _, k=at // size: (0, k))
         specs = [
             pl.BlockSpec((1, span), lambda _, k=at // size: (0, k)),
-            whole((tokens, keys)),
-            pl.BlockSpec((span, keys), lambda _, k=at // size: (k, 0)),
+            near,
             whole((tokens, span)),
         ]
         held = () if upper is None else (upper,)
@@ -322,10 +328,10 @@
             in_specs=specs + [pl.BlockSpec(memory_space=pl.ANY)] * len(held),
             out_specs=block,
             out_shape=jax.ShapeDtypeStruct((tokens, wide), bf16),
-            input_output_aliases={4: 0} if held else {},
+            input_output_aliases={3: 0} if held else {},
             compiler_params=order,
             name="upper",
-        )(gate_row, grads, weights, received[n], *held)
+        )(gate_far, branches[n], received[n], *held)
     return (upper[None], basis_t.T[None], q_t.T[None], error_next[None, None])
 
 

time: 100 us -> 107 us (1.070)
  waiting for transfers between devices: 31 us -> 42.8 us
  local copies, waits for them, and re-layouts: 6.65 us -> 1.97 us
  Pallas kernels: 43.9 us -> 42.8 us
    ppermute x3 -> x4, waiting for transfers between devices: 9.48 us -> 20.9 us  [step(): received.append(lax.ppermute(current, 'section', route))]
    unnamed x12 -> x6, local copies, waits for them, and re-layouts: 6.64 us -> 1.96 us
    pallas_call x3 -> x4, Pallas kernels: 10.7 us -> 7.05 us  [step(): pl.pallas_call(upper_kernel, grid=(1,), in_specs=specs + [pl.BlockSpec(me...]
    pallas_call x3 -> x4, Pallas kernels: 7.73 us -> 9.59 us  [step(): pl.pallas_call(branch_kernel, grid=(1,), in_specs=[pl.BlockSpec((1, span)...]
    ppermute x3 -> x4, starting transfers between devices: 4.06 us -> 5.48 us  [step(): received.append(lax.ppermute(current, 'section', route))]
    pallas_call x1, Pallas kernels: 6.78 us -> 7.98 us  [step(): pl.pallas_call(functools.partial(left_kernel, scale=scale, steps=left_ste...]
  transfers between devices with their start and end apart: 14 -> 15, of which waited for: 9 -> 10; matrix products, arithmetic and copies ran while one was open for 0% -> 0% of each run, Pallas kernels for 34% -> 31%
where the time goes in v3:
time: 107 us
  Pallas kernels  42.8 us (40%)
  waiting for transfers between devices  42.8 us (40%)
  starting transfers between devices  17.9 us (17%)
  local copies, waits for them, and re-layouts  1.97 us (2%)
    ppermute x11, waiting for transfers between devices, flip(): return lax.ppermute(x, 'dp', [(i, i ^ 1 << bit) for i in range(n)])  21.9 us
    ppermute x4, waiting for transfers between devices, step(): received.append(lax.ppermute(current, 'section', route))  20.9 us
    ppermute x11, starting transfers between devices, flip(): return lax.ppermute(x, 'dp', [(i, i ^ 1 << bit) for i in range(n)])  12.5 us
    pallas_call x4, Pallas kernels, step(): pl.pallas_call(branch_kernel, grid=(1,), in_specs=[pl.BlockSpec((1, span)...  9.59 us
    pallas_call x1, Pallas kernels, step(): pl.pallas_call(functools.partial(left_kernel, scale=scale, steps=left_ste...  7.98 us
    pallas_call x4, Pallas kernels, step(): pl.pallas_call(upper_kernel, grid=(1,), in_specs=specs + [pl.BlockSpec(me...  7.05 us
    pallas_call x1, Pallas kernels, step(): pl.pallas_call(functools.partial(final_kernel, halves=2), grid=(unit_step...  5.59 us
    ppermute x4, starting transfers between devices, step(): received.append(lax.ppermute(current, 'section', route))  5.48 us
  transfers between devices with their start and end apart: 15, of which 10 were waited for; matrix products, arithmetic and copies ran while one was open for 0% of the time, Pallas kernels for 31%

profile of v3, /device:TPU:0, one launch (start us, length us, event | category | flops | bytes accessed | tf_op | source)
XLA Modules:
  0.0 106.5 jit_solution(14336358996309867409)
XLA Ops:
  0.6 0.1 pad_add_fusion.me_ref
  0.7 0.0 copy-start
  0.7 1.1 copy-done
  1.8 0.0 copy-start.2
  1.8 0.9 copy-done.2
  2.7 8.0 %left.1 = (f32[16,4096]{1,0:T(8,128)S(1)}, f32[16,4096]{1,0:T(8,128)S(1)}, bf16[384,4096]{1,0:T(8,128)(2,1)S(1)}, bf16[4096,768]{1,0:T(8,128)(2,1)S(1)}) custom-call(s32[2]{0:T(128)S(1)} %pad_add_fusion.me_ref, f32[32,768]{1,0:T(8,128)S(1)} %bitcast.25, bf16[384,768]{1,0:T(8,128)(2,1)S(1)} %bitcast.21, bf16[384,4096]{1,0:T(8,128)(2,1)} %bitcast.32, ...), custom_call_target="tpu_custom_call" | custom-call | tf_op jit(solution)/shard_map/left/pallas_call | solution.py:233
  10.7 0.6 collective-permute-start.4
  11.2 1.2 %collective-permute-done.4 = f32[16,4096]{1,0:T(8,128)S(1)} collective-permute-done((f32[16,4096]{1,0:T(8,128)S(1)}, f32[16,4096]{1,0:T(8,128)S(1)}, u32[]{:S(2)}, u32[]{:S(2)}) %collective-permute-start.4) | collective-permute-done | bytes 262176 | tf_op jit(solution)/shard_map/ppermute | solution.py:180
  12.4 2.9 %collective-permute-start.5 = (f32[8,4096]{1,0:T(8,128)S(1)}, f32[8,4096]{1,0:T(8,128)S(1)}, u32[]{:S(2)}, u32[]{:S(2)}) collective-permute-start(f32[8,4096]{1,0:T(8,128)S(1)} %slice.9), channel_id=1, source_target_pairs={{0,2},{1,3},{2,0},{3,1},{4,6},{5,7},{6,4},{7,5},{8,10},{9,11},{10,... | collective-permute-start | bytes 393224 | tf_op jit(solution)/shard_map/ppermute | solution.py:180
  15.4 3.5 %branch.5 = (bf16[384,2048]{1,0:T(8,128)(2,1)S(1)}, f32[384,2048]{1,0:T(8,128)S(1)}) custom-call(f32[1,4096]{1,0:T(1,128)} %gate_ref.15, bf16[384,768]{1,0:T(8,128)(2,1)} %bitcast.17, bf16[4096,768]{1,0:T(8,128)(2,1)} %bitcast.26), custom_call_target="tpu_custom_call" | custom-call | tf_op jit(solution)/shard_map/branch/pallas_call | solution.py:215
  18.9 1.3 %collective-permute-start.1 = (bf16[384,2048]{1,0:T(8,128)(2,1)S(1)}, bf16[384,2048]{1,0:T(8,128)(2,1)S(1)}, u32[]{:S(2)}, u32[]{:S(2)}) collective-permute-start(bf16[384,2048]{1,0:T(8,128)(2,1)S(1)} %get-tuple-element.26), channel_id=1, source_target_pairs={{16,0},{17,1},{18,2},{19,3},{20,4},{21,5},{22,6},{23,7},{24,8},{25... | collective-permute-start | bytes 4718600 | tf_op jit(solution)/shard_map/ppermute | solution.py:229
  20.2 0.0 collective-permute-done.5
  20.2 1.6 %collective-permute-start.6 = (f32[8,4096]{1,0:T(8,128)S(1)}, f32[8,4096]{1,0:T(8,128)S(1)}, u32[]{:S(2)}, u32[]{:S(2)}) collective-permute-start(f32[8,4096]{1,0:T(8,128)S(1)} %slice_add_fusion), channel_id=1, source_target_pairs={{0,4},{1,5},{2,6},{3,7},{4,0},{5,1},{6,2},{7,3},{8,12},{9,13},{10,... | collective-permute-start | bytes 393224 | tf_op jit(solution)/shard_map/ppermute | solution.py:180
  21.9 3.7 %collective-permute-done.6 = f32[8,4096]{1,0:T(8,128)S(1)} collective-permute-done((f32[8,4096]{1,0:T(8,128)S(1)}, f32[8,4096]{1,0:T(8,128)S(1)}, u32[]{:S(2)}, u32[]{:S(2)}) %collective-permute-start.6) | collective-permute-done | bytes 131104 | tf_op jit(solution)/shard_map/ppermute | solution.py:180
  25.6 2.7 %collective-permute-start.7 = (f32[8,4096]{1,0:T(8,128)S(1)}, f32[8,4096]{1,0:T(8,128)S(1)}, u32[]{:S(2)}, u32[]{:S(2)}) collective-permute-start(f32[8,4096]{1,0:T(8,128)S(1)} %add.26), channel_id=1, source_target_pairs={{0,8},{1,9},{2,10},{3,11},{4,12},{5,13},{6,14},{7,15},{8,0},{9,1},... | collective-permute-start | bytes 393224 | tf_op jit(solution)/shard_map/ppermute | solution.py:180
  28.2 5.5 %collective-permute-done.7 = f32[8,4096]{1,0:T(8,128)S(1)} collective-permute-done((f32[8,4096]{1,0:T(8,128)S(1)}, f32[8,4096]{1,0:T(8,128)S(1)}, u32[]{:S(2)}, u32[]{:S(2)}) %collective-permute-start.7) | collective-permute-done | bytes 131104 | tf_op jit(solution)/shard_map/ppermute | solution.py:180
  33.8 0.3 collective-permute-start.8
  34.1 2.4 %branch.4 = (bf16[384,1024]{1,0:T(8,128)(2,1)S(1)}, f32[384,1024]{1,0:T(8,128)S(1)}) custom-call(f32[1,4096]{1,0:T(1,128)} %gate_ref.15, bf16[384,768]{1,0:T(8,128)(2,1)} %bitcast.18, bf16[4096,768]{1,0:T(8,128)(2,1)} %bitcast.27), custom_call_target="tpu_custom_call" | custom-call | tf_op jit(solution)/shard_map/branch/pallas_call | solution.py:215
  36.5 1.3 %collective-permute-start = (bf16[384,1024]{1,0:T(8,128)(2,1)S(1)}, bf16[384,1024]{1,0:T(8,128)(2,1)S(1)}, u32[]{:S(2)}, u32[]{:S(2)}) collective-permute-start(bf16[384,1024]{1,0:T(8,128)(2,1)S(1)} %get-tuple-element.24), channel_id=1, source_target_pairs={{16,0},{17,1},{18,2},{19,3},{20,4},{21,5},{22,6},{23,7},{24,8},{25... | collective-permute-start | bytes 2359304 | tf_op jit(solution)/shard_map/ppermute | solution.py:229
  37.8 1.0 collective-permute-done.8.py_ref
  38.8 0.1 collective-permute-start.9
  38.9 1.8 %branch.7 = (bf16[384,512]{1,0:T(8,128)(2,1)S(1)}, f32[384,512]{1,0:T(8,128)S(1)}) custom-call(f32[1,4096]{1,0:T(1,128)} %gate_ref.15, bf16[384,768]{1,0:T(8,128)(2,1)} %bitcast.19, bf16[4096,768]{1,0:T(8,128)(2,1)} %bitcast.28), custom_call_target="tpu_custom_call" | custom-call | tf_op jit(solution)/shard_map/branch/pallas_call | solution.py:215
  40.7 0.0 copy-start.1
  40.7 1.4 %collective-permute-start.3 = (bf16[384,512]{1,0:T(8,128)(2,1)S(1)}, bf16[384,512]{1,0:T(8,128)(2,1)S(1)}, u32[]{:S(2)}, u32[]{:S(2)}) collective-permute-start(bf16[384,512]{1,0:T(8,128)(2,1)S(1)} %get-tuple-element.30), channel_id=1, source_target_pairs={{16,0},{17,1},{18,2},{19,3},{20,4},{21,5},{22,6},{23,7},{24,8},{25... | collective-permute-start | bytes 1179656 | tf_op jit(solution)/shard_map/ppermute | solution.py:229
  42.2 1.8 %branch.6 = (bf16[384,512]{1,0:T(8,128)(2,1)S(1)}, f32[384,512]{1,0:T(8,128)S(1)}) custom-call(f32[1,4096]{1,0:T(1,128)} %gate_ref.15, bf16[384,768]{1,0:T(8,128)(2,1)} %bitcast.20, bf16[4096,768]{1,0:T(8,128)(2,1)} %bitcast.29), custom_call_target="tpu_custom_call" | custom-call | tf_op jit(solution)/shard_map/branch/pallas_call | solution.py:215
  44.0 1.5 %collective-permute-start.2 = (bf16[384,512]{1,0:T(8,128)(2,1)S(1)}, bf16[384,512]{1,0:T(8,128)(2,1)S(1)}, u32[]{:S(2)}, u32[]{:S(2)}) collective-permute-start(bf16[384,512]{1,0:T(8,128)(2,1)S(1)} %get-tuple-element.28), channel_id=1, source_target_pairs={{16,0},{17,1},{18,2},{19,3},{20,4},{21,5},{22,6},{23,7},{24,8},{25... | collective-permute-start | bytes 1179656 | tf_op jit(solution)/shard_map/ppermute | solution.py:229
  45.5 0.0 collective-permute-done.9.pc_ref
  45.5 0.0 copy-done.1
  45.5 4.1 %right.1 = (f32[16,768]{1,0:T(8,128)S(1)}, f32[16,768]{1,0:T(8,128)S(1)}, f32[96,96]{1,0:T(8,128)S(1)}) custom-call(s32[2]{0:T(128)S(1)} %pad_add_fusion.me_ref, f32[8,4096]{1,0:T(8,128)S(1)} %add.27.pm_ref, f32[8,4096]{1,0:T(8,128)S(1)} %collective-permute-done.8.py_ref, f32[16,4096]{1,0:T(8,128)S(1)} %collective-permute-done.9.pc_ref, ...), custom_call_target="tpu_custom_call" | custom-call | tf_op jit(solution)/shard_map/right/pallas_call | solution.py:269
  49.7 0.6 collective-permute-start.10
  50.2 0.9 collective-permute-done.10
  51.1 0.8 collective-permute-start.11
  51.9 3.3 %collective-permute-done.11 = f32[16,768]{1,0:T(8,128)S(1)} collective-permute-done((f32[16,768]{1,0:T(8,128)S(1)}, f32[16,768]{1,0:T(8,128)S(1)}, u32[]{:S(2)}, u32[]{:S(2)}) %collective-permute-start.11) | collective-permute-done | bytes 49184 | tf_op jit(solution)/shard_map/ppermute | solution.py:180
  55.2 0.7 collective-permute-start.12
  55.9 3.4 %collective-permute-done.12 = f32[16,768]{1,0:T(8,128)S(1)} collective-permute-done((f32[16,768]{1,0:T(8,128)S(1)}, f32[16,768]{1,0:T(8,128)S(1)}, u32[]{:S(2)}, u32[]{:S(2)}) %collective-permute-start.12) | collective-permute-done | bytes 49184 | tf_op jit(solution)/shard_map/ppermute | solution.py:180
  59.4 2.1 %collective-permute-start.13 = (f32[16,768]{1,0:T(8,128)S(1)}, f32[16,768]{1,0:T(8,128)S(1)}, u32[]{:S(2)}, u32[]{:S(2)}) collective-permute-start(f32[16,768]{1,0:T(8,128)S(1)} %add.30), channel_id=1, source_target_pairs={{0,8},{1,9},{2,10},{3,11},{4,12},{5,13},{6,14},{7,15},{8,0},{9,1},... | collective-permute-start | bytes 147464 | tf_op jit(solution)/shard_map/ppermute | solution.py:180
  61.5 2.9 %collective-permute-done.13 = f32[16,768]{1,0:T(8,128)S(1)} collective-permute-done((f32[16,768]{1,0:T(8,128)S(1)}, f32[16,768]{1,0:T(8,128)S(1)}, u32[]{:S(2)}, u32[]{:S(2)}) %collective-permute-start.13) | collective-permute-done | bytes 49184 | tf_op jit(solution)/shard_map/ppermute | solution.py:180
  64.4 0.1 collective-permute-start.14
  64.5 1.8 %merged.2.rest_0_ = f32[2048,768]{1,0:T(8,128)S(1)} custom-call(bf16[384,4096]{1,0:T(8,128)(2,1)S(1)} %get-tuple-element.33.x_ref, bf16[384,768]{1,0:T(8,128)(2,1)S(1)} %bitcast.23, bf16[4096,768]{1,0:T(8,128)(2,1)S(1)} %get-tuple-element.34.e_ref), custom_call_target="tpu_custom_call" | custom-call | tf_op jit(solution)/shard_map/merged/pallas_call | solution.py:259
  66.3 1.8 %merged.3.rest_1_ = f32[2048,768]{1,0:T(8,128)S(1)} custom-call(bf16[384,4096]{1,0:T(8,128)(2,1)S(1)} %get-tuple-element.33.x_ref, bf16[384,768]{1,0:T(8,128)(2,1)S(1)} %bitcast.24, bf16[4096,768]{1,0:T(8,128)(2,1)S(1)} %get-tuple-element.34.e_ref), custom_call_target="tpu_custom_call" | custom-call | tf_op jit(solution)/shard_map/merged/pallas_call | solution.py:259
  68.2 15.1 %collective-permute-done.3.c_ref = bf16[384,512]{1,0:T(8,128)(2,1)S(1)} collective-permute-done((bf16[384,512]{1,0:T(8,128)(2,1)S(1)}, bf16[384,512]{1,0:T(8,128)(2,1)S(1)}, u32[]{:S(2)}, u32[]{:S(2)}) %collective-permute-start.3) | collective-permute-done | bytes 393248 | tf_op jit(solution)/shard_map/ppermute | solution.py:229
  83.3 1.5 %upper.4.rest_0_ = bf16[384,4096]{1,0:T(8,128)(2,1)} custom-call(f32[1,4096]{1,0:T(1,128)} %gate_ref.15, f32[384,512]{1,0:T(8,128)S(1)} %get-tuple-element.29.branch_ref, bf16[384,512]{1,0:T(8,128)(2,1)S(1)} %collective-permute-done.3.c_ref), custom_call_target="tpu_custom_call" | custom-call | tf_op jit(solution)/shard_map/upper/pallas_call | solution.py:325
  84.9 5.8 %collective-permute-done.2.c_ref = bf16[384,512]{1,0:T(8,128)(2,1)S(1)} collective-permute-done((bf16[384,512]{1,0:T(8,128)(2,1)S(1)}, bf16[384,512]{1,0:T(8,128)(2,1)S(1)}, u32[]{:S(2)}, u32[]{:S(2)}) %collective-permute-start.2) | collective-permute-done | bytes 393248 | tf_op jit(solution)/shard_map/ppermute | solution.py:229
  90.6 1.5 %upper.5.rest_0_ = bf16[384,4096]{1,0:T(8,128)(2,1)} custom-call(f32[1,4096]{1,0:T(1,128)} %gate_ref.15, f32[384,512]{1,0:T(8,128)S(1)} %get-tuple-element.27.branch_ref, bf16[384,512]{1,0:T(8,128)(2,1)S(1)} %collective-permute-done.2.c_ref, bf16[384,4096]{1,0:T(8,128)(2,1)} %upper.4.rest_0_), custom_call_target="tpu_custom_call", output_to_operand_aliasing={{}: (3, {})} | custom-call | tf_op jit(solution)/shard_map/upper/pallas_call | solution.py:325
  92.2 2.8 %factor.1.inv_ref = f32[32,32]{1,0:T(8,128)S(1)} custom-call(f32[96,96]{1,0:T(8,128)S(1)} %get-tuple-element.35.gram_ref), custom_call_target="tpu_custom_call" | custom-call | tf_op jit(solution)/shard_map/factor/pallas_call | solution.py:284
  95.0 2.0 %basis.1 = (f32[32,4096]{1,0:T(8,128)}, bf16[4096,128]{1,0:T(8,128)(2,1)S(1)}) custom-call(s32[2]{0:T(128)S(1)} %pad_add_fusion.me_ref, f32[32,32]{1,0:T(8,128)S(1)} %factor.1.inv_ref, f32[8,4096]{1,0:T(8,128)S(1)} %add.27.pm_ref, f32[8,4096]{1,0:T(8,128)S(1)} %collective-permute-done.8.py_ref, f32[16,4096]{1,0:T(8,128)S(1)} %collective-permute-done.9.pc_ref), custom_call_target="tpu_custom_call" | custom-call | tf_op jit(solution)/shard_map/basis/pallas_call | solution.py:291
  96.9 0.0 collective-permute-done.14.ro_ref
  96.9 5.6 %final.1 = (bf16[4096,768]{1,0:T(8,128)(2,1)}, f32[32,768]{1,0:T(8,128)}) custom-call(s32[2]{0:T(128)S(1)} %pad_add_fusion.me_ref, f32[32,32]{1,0:T(8,128)S(1)} %factor.1.inv_ref, f32[16,768]{1,0:T(8,128)S(1)} %add.31.rk_ref, f32[16,768]{1,0:T(8,128)S(1)} %collective-permute-done.14.ro_ref, bf16[4096,128]{1,0:T(8,128)(2,1)S(1)} %get-tuple-element.39.terms_ref, ...), custom_call_target="tpu_custom_call" | custom-call | tf_op jit(solution)/shard_map/final/pallas_call | solution.py:301
  102.5 0.0 collective-permute-done.1.c_ref
  102.5 2.2 %upper.6.rest_0_ = bf16[384,4096]{1,0:T(8,128)(2,1)} custom-call(f32[1,4096]{1,0:T(1,128)} %gate_ref.15, f32[384,2048]{1,0:T(8,128)S(1)} %get-tuple-element.25.branch_ref, bf16[384,2048]{1,0:T(8,128)(2,1)S(1)} %collective-permute-done.1.c_ref, bf16[384,4096]{1,0:T(8,128)(2,1)} %upper.5.rest_0_), custom_call_target="tpu_custom_call", output_to_operand_aliasing={{}: (3, {})} | custom-call | tf_op jit(solution)/shard_map/upper/pallas_call | solution.py:325
  104.7 0.0 collective-permute-done.c_ref
  104.7 1.8 %upper.7 = bf16[384,4096]{1,0:T(8,128)(2,1)} custom-call(f32[1,4096]{1,0:T(1,128)} %gate_ref.15, f32[384,1024]{1,0:T(8,128)S(1)} %get-tuple-element.23.branch_ref, bf16[384,1024]{1,0:T(8,128)(2,1)S(1)} %collective-permute-done.c_ref, bf16[384,4096]{1,0:T(8,128)(2,1)} %upper.6.rest_0_), custom_call_target="tpu_custom_call", output_to_operand_aliasing={{}: (3, {})} | custom-call | tf_op jit(solution)/shard_map/upper/pallas_call | solution.py:325
  (10 shorter events, 0.1 us)
Async XLA Ops:
  0.7 1.1 copy-start
  1.8 0.9 copy-start.2
  10.7 1.7 %collective-permute-start.4 = (f32[16,4096]{1,0:T(8,128)S(1)}, f32[16,4096]{1,0:T(8,128)S(1)}, u32[]{:S(2)}, u32[]{:S(2)}) collective-permute-start(f32[16,4096]{1,0:T(8,128)S(1)} %get-tuple-element.32), channel_id=1, source_target_pairs={{0,1},{1,0},{2,3},{3,2},{4,5},{5,4},{6,7},{7,6},{8,9},{9,8},{10,11... | collective-permute-start | bytes 786440 | tf_op jit(solution)/shard_map/ppermute | solution.py:180
  12.4 7.8 %collective-permute-start.5 = (f32[8,4096]{1,0:T(8,128)S(1)}, f32[8,4096]{1,0:T(8,128)S(1)}, u32[]{:S(2)}, u32[]{:S(2)}) collective-permute-start(f32[8,4096]{1,0:T(8,128)S(1)} %slice.9), channel_id=1, source_target_pairs={{0,2},{1,3},{2,0},{3,1},{4,6},{5,7},{6,4},{7,5},{8,10},{9,11},{10,... | collective-permute-start | bytes 393224 | tf_op jit(solution)/shard_map/ppermute | solution.py:180
  18.9 83.6 %collective-permute-start.1 = (bf16[384,2048]{1,0:T(8,128)(2,1)S(1)}, bf16[384,2048]{1,0:T(8,128)(2,1)S(1)}, u32[]{:S(2)}, u32[]{:S(2)}) collective-permute-start(bf16[384,2048]{1,0:T(8,128)(2,1)S(1)} %get-tuple-element.26), channel_id=1, source_target_pairs={{16,0},{17,1},{18,2},{19,3},{20,4},{21,5},{22,6},{23,7},{24,8},{25... | collective-permute-start | bytes 4718600 | tf_op jit(solution)/shard_map/ppermute | solution.py:229
  20.2 5.3 %collective-permute-start.6 = (f32[8,4096]{1,0:T(8,128)S(1)}, f32[8,4096]{1,0:T(8,128)S(1)}, u32[]{:S(2)}, u32[]{:S(2)}) collective-permute-start(f32[8,4096]{1,0:T(8,128)S(1)} %slice_add_fusion), channel_id=1, source_target_pairs={{0,4},{1,5},{2,6},{3,7},{4,0},{5,1},{6,2},{7,3},{8,12},{9,13},{10,... | collective-permute-start | bytes 393224 | tf_op jit(solution)/shard_map/ppermute | solution.py:180
  25.6 8.2 %collective-permute-start.7 = (f32[8,4096]{1,0:T(8,128)S(1)}, f32[8,4096]{1,0:T(8,128)S(1)}, u32[]{:S(2)}, u32[]{:S(2)}) collective-permute-start(f32[8,4096]{1,0:T(8,128)S(1)} %add.26), channel_id=1, source_target_pairs={{0,8},{1,9},{2,10},{3,11},{4,12},{5,13},{6,14},{7,15},{8,0},{9,1},... | collective-permute-start | bytes 393224 | tf_op jit(solution)/shard_map/ppermute | solution.py:180
  33.8 5.0 %collective-permute-start.8 = (f32[8,4096]{1,0:T(8,128)S(1)}, f32[8,4096]{1,0:T(8,128)S(1)}, u32[]{:S(2)}, u32[]{:S(2)}) collective-permute-start(f32[8,4096]{1,0:T(8,128)S(1)} %add.27.pm_ref), channel_id=1, source_target_pairs={{0,2},{1,3},{2,0},{3,1},{4,6},{5,7},{6,4},{7,5},{8,10},{9,11},{10,... | collective-permute-start | bytes 393224 | tf_op jit(solution)/shard_map/ppermute | solution.py:180
  36.5 68.2 %collective-permute-start = (bf16[384,1024]{1,0:T(8,128)(2,1)S(1)}, bf16[384,1024]{1,0:T(8,128)(2,1)S(1)}, u32[]{:S(2)}, u32[]{:S(2)}) collective-permute-start(bf16[384,1024]{1,0:T(8,128)(2,1)S(1)} %get-tuple-element.24), channel_id=1, source_target_pairs={{16,0},{17,1},{18,2},{19,3},{20,4},{21,5},{22,6},{23,7},{24,8},{25... | collective-permute-start | bytes 2359304 | tf_op jit(solution)/shard_map/ppermute | solution.py:229
  38.8 6.7 %collective-permute-start.9 = (f32[16,4096]{1,0:T(8,128)S(1)}, f32[16,4096]{1,0:T(8,128)S(1)}, u32[]{:S(2)}, u32[]{:S(2)}) collective-permute-start(f32[16,4096]{1,0:T(8,128)S(1)} %pad_maximum_fusion), channel_id=1, source_target_pairs={{0,1},{1,0},{2,3},{3,2},{4,5},{5,4},{6,7},{7,6},{8,9},{9,8},{10,11... | collective-permute-start | bytes 786440 | tf_op jit(solution)/shard_map/ppermute | solution.py:180
  40.7 4.8 %copy-start.1 = (bf16[1,384,768]{2,1,0:T(8,128)(2,1)S(1)}, bf16[1,384,768]{2,1,0:T(8,128)(2,1)}, u32[]{:S(2)}) copy-start(bf16[1,384,768]{2,1,0:T(8,128)(2,1)} %param.7) | copy-start | bytes 1769476
  40.7 42.6 %collective-permute-start.3 = (bf16[384,512]{1,0:T(8,128)(2,1)S(1)}, bf16[384,512]{1,0:T(8,128)(2,1)S(1)}, u32[]{:S(2)}, u32[]{:S(2)}) collective-permute-start(bf16[384,512]{1,0:T(8,128)(2,1)S(1)} %get-tuple-element.30), channel_id=1, source_target_pairs={{16,0},{17,1},{18,2},{19,3},{20,4},{21,5},{22,6},{23,7},{24,8},{25... | collective-permute-start | bytes 1179656 | tf_op jit(solution)/shard_map/ppermute | solution.py:229
  44.0 46.6 %collective-permute-start.2 = (bf16[384,512]{1,0:T(8,128)(2,1)S(1)}, bf16[384,512]{1,0:T(8,128)(2,1)S(1)}, u32[]{:S(2)}, u32[]{:S(2)}) collective-permute-start(bf16[384,512]{1,0:T(8,128)(2,1)S(1)} %get-tuple-element.28), channel_id=1, source_target_pairs={{16,0},{17,1},{18,2},{19,3},{20,4},{21,5},{22,6},{23,7},{24,8},{25... | collective-permute-start | bytes 1179656 | tf_op jit(solution)/shard_map/ppermute | solution.py:229
  49.7 1.4 %collective-permute-start.10 = (f32[16,768]{1,0:T(8,128)S(1)}, f32[16,768]{1,0:T(8,128)S(1)}, u32[]{:S(2)}, u32[]{:S(2)}) collective-permute-start(f32[16,768]{1,0:T(8,128)S(1)} %get-tuple-element.38), channel_id=1, source_target_pairs={{0,1},{1,0},{2,3},{3,2},{4,5},{5,4},{6,7},{7,6},{8,9},{9,8},{10,11... | collective-permute-start | bytes 147464 | tf_op jit(solution)/shard_map/ppermute | solution.py:180
  51.1 4.1 %collective-permute-start.11 = (f32[16,768]{1,0:T(8,128)S(1)}, f32[16,768]{1,0:T(8,128)S(1)}, u32[]{:S(2)}, u32[]{:S(2)}) collective-permute-start(f32[16,768]{1,0:T(8,128)S(1)} %add.28), channel_id=1, source_target_pairs={{0,2},{1,3},{2,0},{3,1},{4,6},{5,7},{6,4},{7,5},{8,10},{9,11},{10,... | collective-permute-start | bytes 147464 | tf_op jit(solution)/shard_map/ppermute | solution.py:180
  55.2 4.1 %collective-permute-start.12 = (f32[16,768]{1,0:T(8,128)S(1)}, f32[16,768]{1,0:T(8,128)S(1)}, u32[]{:S(2)}, u32[]{:S(2)}) collective-permute-start(f32[16,768]{1,0:T(8,128)S(1)} %add.29), channel_id=1, source_target_pairs={{0,4},{1,5},{2,6},{3,7},{4,0},{5,1},{6,2},{7,3},{8,12},{9,13},{10,... | collective-permute-start | bytes 147464 | tf_op jit(solution)/shard_map/ppermute | solution.py:180
  59.4 5.0 %collective-permute-start.13 = (f32[16,768]{1,0:T(8,128)S(1)}, f32[16,768]{1,0:T(8,128)S(1)}, u32[]{:S(2)}, u32[]{:S(2)}) collective-permute-start(f32[16,768]{1,0:T(8,128)S(1)} %add.30), channel_id=1, source_target_pairs={{0,8},{1,9},{2,10},{3,11},{4,12},{5,13},{6,14},{7,15},{8,0},{9,1},... | collective-permute-start | bytes 147464 | tf_op jit(solution)/shard_map/ppermute | solution.py:180
  64.4 32.5 %collective-permute-start.14 = (f32[16,768]{1,0:T(8,128)S(1)}, f32[16,768]{1,0:T(8,128)S(1)}, u32[]{:S(2)}, u32[]{:S(2)}) collective-permute-start(f32[16,768]{1,0:T(8,128)S(1)} %add.31.rk_ref), channel_id=1, source_target_pairs={{0,1},{1,0},{2,3},{3,2},{4,5},{5,4},{6,7},{7,6},{8,9},{9,8},{10,11... | collective-permute-start | bytes 147464 | tf_op jit(solution)/shard_map/ppermute | solution.py:180
